TPU v7x, 256 devices: a whole 4x4x8 slice. The times are simulated.
256 devices in a mesh: tm: 8 (over z_lo, core), space: 32 (over z_hi, x, y).
Axes of the slice: x: 4, y: 4, z: 8 (z_hi: 2, z_lo: 4; z = z_hi * 4 + z_lo), core: 2. Of those that a mesh axis runs over, the one named last changes fastest.
Arguments:
- field_a: float32 [8, 8, 96, 18432], P('tm', None, 'space'), may hold values from -6 to 6
- field_b: float32 [8, 8, 96, 18432], P('tm', None, 'space'), may hold values from -6 to 6
- pairs: int32 [4, 16, 2], replicated, may hold values from 0 to 7
- signs: int32 [4, 16], replicated, may hold values from -1 to 1, as said below
Outputs:
- correlator: float32 [8, 4, 96, 18432], P('tm', None, 'space')
- first_diff: float32 [8, 4, 96, 18432], P('tm', None, 'space')
- second_diff: float32 [8, 4, 96, 18432], P('tm', None, 'space')
Inputs may be any that keep to these rules, and one draw needn't show every extreme that they name: `signs`: each coefficient is -1 or 1.
All inputs are finite; a program needn't handle non-finite values.
Results may differ from a plain program's by a relative error of at most 0.0001.
Values sent between devices are 32-bit elements; how exact they have to be, the bound alone decides.
A program may use at most 192 MiB of HBM per device.

v0:
```python
import math

import jax
import jax.numpy as jnp
from jax import lax
from jax.sharding import PartitionSpec as P

NZ = 96


highest = lax.Precision.HIGHEST


def padded_2(value, sides, width):
    for axis, dim in sides:
        devices, length = (lax.axis_size(axis), value.shape[dim])
        up = [(i, (i + 1) % devices) for i in range(devices)]
        down = [(j, i) for i, j in up]
        last = lax.slice_in_dim(value, length - width, length, axis=dim)
        leading = lax.slice_in_dim(value, 0, width, axis=dim)
        before = lax.ppermute(last, axis, up)
        after = lax.ppermute(leading, axis, down)
        value = jnp.concatenate([before, value, after], axis=dim)
    return value


def dft_tables(length):
    index = jnp.arange(length, dtype=jnp.int32)
    product = index[:, None] * index[None, :] % length
    angle = product.astype(jnp.float32) * (2.0 * math.pi / length)
    norm_scale = 1.0 / math.sqrt(length)
    return (jnp.cos(angle) * norm_scale, jnp.sin(angle) * norm_scale)


def as_five(values):
    return values.reshape(values.shape[:3] + (-1, 2 * NZ))


def as_four(values):
    return values.reshape(values.shape[:3] + (-1,))


def swap_parts(values):
    half = values.shape[-1] // 2
    return jnp.concatenate([values[..., half:], -values[..., :half]], axis=-1)


def along_depth(values, inverse):
    cosines, sines = dft_tables(values.shape[-1] // 2)
    matrix = jnp.block([[cosines, -sines], [sines, cosines]])
    if inverse:
        return jnp.einsum("tcxyr,kr->tcxyk", values, matrix, precision=highest)
    return jnp.einsum("tcxyr,rk->tcxyk", values, matrix, precision=highest)


def along_rows(values, sign):
    cosines, sines = dft_tables(values.shape[3])
    table = jnp.concatenate([cosines, sign * sines], axis=1)
    stacked = jnp.concatenate([values, swap_parts(values)], axis=3)
    return jnp.einsum("ky,tcxyr->tcxkr", table, stacked, precision=highest)


def along_columns(values, sign):
    cosines, sines = dft_tables(values.shape[2])
    table = jnp.concatenate([cosines, sign * sines], axis=1)
    stacked = jnp.concatenate([values, swap_parts(values)], axis=2)
    return jnp.einsum("kx,tcxyr->tckyr", table, stacked, precision=highest)


def contract(weights, hat_a, hat_b):
    depth = hat_a.shape[-1] // 2
    outputs = []
    for channel in range(weights.shape[0]):
        mixed_b = jnp.einsum("ij,tjxyk->tixyk", weights[channel], hat_b, precision=highest)
        direct = jnp.sum(hat_a * mixed_b, axis=1)
        crossed = jnp.sum(hat_a * swap_parts(mixed_b), axis=1)
        real_part = direct[..., :depth] + direct[..., depth:]
        imag_part = -(crossed[..., :depth] + crossed[..., depth:])
        outputs.append(jnp.concatenate([real_part, imag_part], axis=-1))
    return jnp.stack(outputs, axis=1)


def per_device(field_a, field_b, pairs, signs):
    components = field_a.shape[1]
    indices = jnp.arange(components, dtype=jnp.int32)
    first = (pairs[:, :, 0][:, :, None] == indices[None, None, :]).astype(jnp.float32)
    second = (pairs[:, :, 1][:, :, None] == indices[None, None, :]).astype(jnp.float32)
    weights = jnp.einsum(
        "cp,cpi,cpj->cij", signs.astype(jnp.float32), first, second, precision=highest
    )
    partial_a = as_four(along_rows(along_depth(as_five(field_a), False), 1.0))
    partial_b = as_four(along_rows(along_depth(as_five(field_b), False), 1.0))
    lines_a = lax.all_to_all(partial_a, "space", split_axis=3, concat_axis=2, tiled=True)
    lines_b = lax.all_to_all(partial_b, "space", split_axis=3, concat_axis=2, tiled=True)
    hat_a = along_columns(as_five(lines_a), 1.0)
    hat_b = along_columns(as_five(lines_b), 1.0)
    returned = as_four(along_columns(contract(weights, hat_a, hat_b), -1.0))
    mixed_sites = lax.all_to_all(returned, "space", split_axis=2, concat_axis=3, tiled=True)
    correlator = as_four(along_depth(along_rows(as_five(mixed_sites), -1.0), True))
    padded = padded_2(correlator, (("tm", 0),), 1)
    later = padded[2:]
    earlier = padded[:-2]
    first_diff = later - correlator
    second_diff = later - 2.0 * correlator + earlier
    return (correlator, first_diff, second_diff)


def solution(mesh):
    return jax.shard_map(
        per_device,
        mesh=mesh,
        in_specs=(P("tm", None, "space", None), P("tm", None, "space", None), P(), P()),
        out_specs=(
            P("tm", None, "space", None),
            P("tm", None, "space", None),
            P("tm", None, "space", None),
        ),
        check_vma=False,
    )
```

profile of v0, /device:TPU:1, one launch (start us, length us, event | category | flops | bytes accessed | tf_op | source)
XLA Modules:
  0.0 785.2 jit_solution(7867402153758019469)
XLA Ops:
  6.5 3.9 fusion.49
  14.9 41.1 %copy.115 = f32[1,8,3,18432]{1,0,2,3:T(1,128)} copy(f32[1,8,3,18432]{3,1,2,0:T(8,128)S(1)} %reshape.108) | data formatting | bytes 3538944 | tf_op jit(solution)/shard_map/reshape | solution.py:40
  56.6 96.0 %reduce.8 = f32[18432,3,8]{2,1,0:T(4,128)} reduce(f32[18432,3,1,8]{3,2,1,0:T(1,128)} %bitcast.221, f32[]{:T(128)} %broadcast.46), dimensions={2}, to_apply=%bitcast.211.reduce_sub_computation | reduce | bytes 3538948
  152.6 34.5 %reshape.132 = f32[32,1,13824]{2,1,0:T(1,128)} reshape(f32[18432,3,8]{2,1,0:T(4,128)} %reduce.8) | data formatting | bytes 3538944
  187.0 15.1 %all-to-all-start.1 = ((f32[32,1,13824]{2,1,0:T(1,128)}), f32[32,1,13824]{2,1,0:T(1,128)}, u32[]{:S(2)}, u32[]{:S(2)}) async-start(f32[32,1,13824]{2,1,0:T(1,128)} %reshape.132), calls=%async_computation.1 | async-start | bytes 3538944 | tf_op jit(solution)/shard_map/all_to_all | solution.py:94
  207.5 3.9 fusion.50
  215.9 41.1 %copy.105 = f32[1,8,3,18432]{1,0,2,3:T(1,128)} copy(f32[1,8,3,18432]{3,1,2,0:T(8,128)S(1)} %reshape.103) | data formatting | bytes 3538944 | tf_op jit(solution)/shard_map/reshape | solution.py:40
  257.0 96.0 %reduce.10 = f32[18432,3,8]{2,1,0:T(4,128)} reduce(f32[18432,3,1,8]{3,2,1,0:T(1,128)} %bitcast.222, f32[]{:T(128)} %broadcast.46), dimensions={2}, to_apply=%bitcast.209.reduce_sub_computation | reduce | bytes 3538948
  353.0 34.5 %reshape.130 = f32[32,1,13824]{2,1,0:T(1,128)} reshape(f32[18432,3,8]{2,1,0:T(4,128)} %reduce.10) | data formatting | bytes 3538944
  387.5 12.2 %all-to-all-start = ((f32[32,1,13824]{2,1,0:T(1,128)}), f32[32,1,13824]{2,1,0:T(1,128)}, u32[]{:S(2)}, u32[]{:S(2)}) async-start(f32[32,1,13824]{2,1,0:T(1,128)} %reshape.130), calls=%async_computation | async-start | bytes 3538944 | tf_op jit(solution)/shard_map/all_to_all | solution.py:93
  400.7 6.3 reduce.9
  407.0 54.1 %reshape.133 = f32[18432,3,1,8]{3,2,1,0:T(1,128)} reshape(f32[32,13824]{1,0:T(8,128)S(1)} %reduce.9) | data formatting | bytes 3538944
  461.1 51.3 %copy.116 = f32[1,8,3,18432]{3,1,2,0:T(8,128)} copy(f32[1,8,3,18432]{1,0,2,3:T(1,128)} %bitcast.223) | data formatting | bytes 3538944 | tf_op jit(solution)/shard_map/all_to_all | solution.py:94
  517.2 4.6 reshape.109
  521.8 3.1 copy.120
  525.1 5.4 fusion.48
  533.4 3.5 fusion.90
  536.9 3.5 fusion.91
  540.4 3.6 fusion.92
  544.0 3.5 fusion.93
  547.5 6.5 reduce.11
  554.0 53.9 %reshape.131 = f32[18432,3,1,8]{3,2,1,0:T(1,128)} reshape(f32[32,13824]{1,0:T(8,128)S(1)} %reduce.11) | data formatting | bytes 3538944
  607.9 51.3 %copy.106 = f32[1,8,3,18432]{3,1,2,0:T(8,128)} copy(f32[1,8,3,18432]{1,0,2,3:T(1,128)} %bitcast.224) | data formatting | bytes 3538944 | tf_op jit(solution)/shard_map/all_to_all | solution.py:93
  663.9 4.8 reshape.104
  668.7 3.1 copy.110
  676.9 3.2 copy.127
  680.1 3.2 copy.123
  683.3 3.2 copy.125
  695.4 9.4 %fusion.40 = (f32[96,3,192]{0,2,1:T(8,128)}, f32[96,3,192]{0,2,1:T(8,128)}, f32[96,3,192]{0,2,1:T(8,128)}, f32[96,3,192]{0,2,1:T(8,128)}, f32[96,3,192]{0,2,1:T(...) fusion(f32[96,3,192,8]{0,2,1,3:T(8,128)S(1)} %copy-done.1, ...), kind=kOutput, calls=%fused_computation.54 | convolution fusion | flops 1029408768 | bytes 19537920 | tf_op jit(solution)/shard_map/kx,tcxyr->tckyr/dot_general | solution.py:67
  713.5 29.9 %all_to_all.45 = f32[1,4,96,576]{3,1,0,2:T(4,128)S(1)} all-to-all(f32[1,4,96,576]{3,1,0,2:T(4,128)S(1)} %copy.131), channel_id=1, replica_groups=mesh['tm'=8,'space'=32] {'space'}, dimensions={2} | all-to-all | bytes 1769472 | tf_op jit(solution)/shard_map/all_to_all | solution.py:98
  750.0 13.7 %collective-permute-start.1 = (f32[1,4,3,18432]{3,1,2,0:T(4,128)S(1)}, f32[1,4,3,18432]{3,1,2,0:T(4,128)S(1)}, u32[]{:S(2)}, u32[]{:S(2)}) collective-permute-start(f32[1,4,3,18432]{3,1,2,0:T(4,128)S(1)} %reshape.117), channel_id=1, source_target_pairs={{0,32},{32,64},{64,96},{96,128},{128,160},{160,192},{192,224},{224... | collective-permute-start | bytes 2654216 | tf_op jit(solution)/shard_map/ppermute | solution.py:21
  763.7 18.6 %collective-permute-done.1 = f32[1,4,3,18432]{3,1,2,0:T(4,128)S(1)} collective-permute-done((f32[1,4,3,18432]{3,1,2,0:T(4,128)S(1)}, f32[1,4,3,18432]{3,1,2,0:T(4,128)S(1)}, u32[]{:S(2)}, u32[]{:S(2)}) %collective-permute-start.1) | collective-permute-done | bytes 884768 | tf_op jit(solution)/shard_map/ppermute | solution.py:21
  (97 shorter events, 65.8 us)
Async XLA Ops:
  0.8 203.6 %copy-start.15 = (f32[96,96]{0,1:T(8,128)}, f32[96,96]{0,1:T(8,128)S(1)}, u32[]{:S(2)}) copy-start(f32[96,96]{0,1:T(8,128)S(1)} %fusion.83) | copy-start | bytes 110596
  1.1 524.0 %copy-start.6 = (f32[96,96]{0,1:T(8,128)}, f32[96,96]{0,1:T(8,128)S(1)}, u32[]{:S(2)}) copy-start(f32[96,96]{0,1:T(8,128)S(1)} %get-tuple-element.38) | copy-start | bytes 110596
  1.1 524.0 %copy-start.10 = (f32[96,96]{0,1:T(8,128)}, f32[96,96]{0,1:T(8,128)S(1)}, u32[]{:S(2)}) copy-start(f32[96,96]{0,1:T(8,128)S(1)} %get-tuple-element.39) | copy-start | bytes 110596
  187.0 200.5 %all-to-all-start.1 = ((f32[32,1,13824]{2,1,0:T(1,128)}), f32[32,1,13824]{2,1,0:T(1,128)}, u32[]{:S(2)}, u32[]{:S(2)}) async-start(f32[32,1,13824]{2,1,0:T(1,128)} %reshape.132), calls=%async_computation.1 | async-start | bytes 3538944 | tf_op jit(solution)/shard_map/all_to_all | solution.py:94
  387.5 12.2 %copy-start.19 = (s32[4,16]{1,0:T(4,128)S(1)}, s32[4,16]{1,0:T(4,128)}, u32[]{:S(2)}) copy-start(s32[4,16]{1,0:T(4,128)} %param.7) | copy-start | bytes 772
  387.5 13.1 %copy-start.18 = (s32[4,16,2]{1,2,0:T(2,128)S(1)}, s32[4,16,2]{1,2,0:T(2,128)}, u32[]{:S(2)}) copy-start(s32[4,16,2]{1,2,0:T(2,128)} %param.6) | copy-start | bytes 1540
  387.5 160.0 %all-to-all-start = ((f32[32,1,13824]{2,1,0:T(1,128)}), f32[32,1,13824]{2,1,0:T(1,128)}, u32[]{:S(2)}, u32[]{:S(2)}) async-start(f32[32,1,13824]{2,1,0:T(1,128)} %reshape.130), calls=%async_computation | async-start | bytes 3538944 | tf_op jit(solution)/shard_map/all_to_all | solution.py:93
  671.8 1.4 copy-start.3
  686.5 2.4 copy-start.2
  688.9 1.7 copy-start
  690.6 3.3 copy-start.5
  690.6 3.3 copy-start.7
  690.6 3.3 copy-start.11
  692.2 2.5 copy-start.1
  692.2 3.2 copy-start.4
  704.8 5.1 copy-start.14
  704.8 5.1 copy-start.13
  710.2 0.8 copy-start.17
  743.9 0.8 copy-start.8
  744.4 2.4 copy-start.12
  744.4 2.4 copy-start.16
  750.0 34.8 %copy-start.9 = (f32[1,4,3,18432]{3,1,2,0:T(4,128)}, f32[1,4,3,18432]{3,1,2,0:T(4,128)S(1)}, u32[]{:S(2)}) copy-start(f32[1,4,3,18432]{3,1,2,0:T(4,128)S(1)} %reshape.117) | copy-start | bytes 2654212
  750.0 32.3 %collective-permute-start.1 = (f32[1,4,3,18432]{3,1,2,0:T(4,128)S(1)}, f32[1,4,3,18432]{3,1,2,0:T(4,128)S(1)}, u32[]{:S(2)}, u32[]{:S(2)}) collective-permute-start(f32[1,4,3,18432]{3,1,2,0:T(4,128)S(1)} %reshape.117), channel_id=1, source_target_pairs={{0,32},{32,64},{64,96},{96,128},{128,160},{160,192},{192,224},{224... | collective-permute-start | bytes 2654216 | tf_op jit(solution)/shard_map/ppermute | solution.py:21
  763.7 19.4 %collective-permute-start = (f32[1,4,3,18432]{3,1,2,0:T(4,128)S(1)}, f32[1,4,3,18432]{3,1,2,0:T(4,128)S(1)}, u32[]{:S(2)}, u32[]{:S(2)}) collective-permute-start(f32[1,4,3,18432]{3,1,2,0:T(4,128)S(1)} %reshape.117), channel_id=1, source_target_pairs={{32,0},{64,32},{96,64},{128,96},{160,128},{192,160},{224,192},{0,2... | collective-permute-start | bytes 2654216 | tf_op jit(solution)/shard_map/ppermute | solution.py:22
where the time goes:
time: 799 us; the launch traced here: 785 us
  local copies, waits for them, and re-layouts  424 us (53%)
  other arithmetic  220 us (28%)
  matrix products  49 us (6%)
  starting transfers between devices  41 us (5%)
  blocking collectives  29.9 us (4%)
  waiting for transfers between devices  19.4 us (2%)
    unnamed x2, other arithmetic  192 us
    unnamed x45, local copies, waits for them, and re-layouts  183 us
    reshape x6, local copies, waits for them, and re-layouts, as_four(): return values.reshape(values.shape[:3] + (-1,))  88.1 us
    all_to_all x3, local copies, waits for them, and re-layouts, per_device(): lax.all_to_all(partial_b, 'space', split_axis=3, concat_axis=2, tiled=True)  56.1 us
    all_to_all x3, local copies, waits for them, and re-layouts, per_device(): lax.all_to_all(partial_a, 'space', split_axis=3, concat_axis=2, tiled=True)  56 us
    all_to_all x1, blocking collectives, per_device(): lax.all_to_all(returned, 'space', split_axis=2, concat_axis=3, tiled=True)  29.9 us
    ppermute x1, waiting for transfers between devices, padded_2(): before = lax.ppermute(last, axis, up)  18.6 us
    dot_general x3, matrix products, along_columns(): return jnp.einsum('kx,tcxyr->tckyr', table, stacked, precision=highest)  16.8 us
  transfers between devices with their start and end apart: 4, of which 2 were waited for; matrix products, arithmetic and copies ran while one was open for 42% of the time, Pallas kernels for 0%

commit v1 on v0

v1 whole, which is shorter than its diff:
```python
import functools
import math

import jax
import jax.numpy as jnp
import ml_dtypes
import numpy as np
from jax import lax
from jax.experimental import pallas as pl
from jax.experimental.pallas import tpu as pltpu
from jax.sharding import PartitionSpec as P

N = 96
PEERS = 32
MESH_ID = pl.DeviceIdType.MESH
F32 = jnp.float32
BF16 = jnp.bfloat16


def halves(table):
    high = table.astype(np.float32).astype(ml_dtypes.bfloat16)
    low = (table - high.astype(np.float64)).astype(np.float32).astype(ml_dtypes.bfloat16)
    return high, low


def trig(out_index, in_index):
    angle = (np.outer(out_index, in_index) % N) * (2.0 * math.pi / N)
    return np.cos(angle) / math.sqrt(N), np.sin(angle) / math.sqrt(N)


def left_table(out_index, in_index, in_parts, forward):
    cosines, sines = trig(out_index, in_index)
    turn = 1.0 if forward else -1.0
    real = np.where(in_parts[None, :] == 0, cosines, turn * sines)
    imag = np.where(in_parts[None, :] == 0, -turn * sines, cosines)
    return np.concatenate(halves(np.concatenate([real, imag], axis=0)), axis=0)


def plain_columns(index):
    return np.concatenate([index, index]), np.repeat([0, 1], N)


def tables():
    sites = np.arange(N)
    pairs_order = np.concatenate([2 * np.arange(48), 2 * np.arange(48) + 1])
    y_in = np.concatenate([2 * np.arange(48) + v for v in (0, 1) for _ in (0, 1)])
    y_parts = np.concatenate([np.full(48, part) for _ in (0, 1) for part in (0, 1)])
    dealt = np.concatenate([3 * np.arange(PEERS) + q for q in range(3)])
    forward_y = left_table(dealt, y_in, y_parts, True)
    forward_x = left_table(sites, *plain_columns(dealt), True)
    inverse_x = left_table(dealt, *plain_columns(sites), False)
    inverse_y = left_table(pairs_order, *plain_columns(dealt), False)
    cosines, sines = trig(sites, sites)
    forward_z = np.zeros((2, 256, 256))
    inverse_z = np.zeros((2, 256, 256))
    for v in (0, 1):
        rows = 64 * v
        forward_z[v, rows : rows + N, 0:N] = cosines
        forward_z[v, rows : rows + N, 128 : 128 + N] = -sines
        forward_z[v, rows + N : rows + 2 * N, 0:N] = sines
        forward_z[v, rows + N : rows + 2 * N, 128 : 128 + N] = cosines
        inverse_z[v, 0:N, rows : rows + N] = cosines
        inverse_z[v, 0:N, rows + N : rows + 2 * N] = sines
        inverse_z[v, 128 : 128 + N, rows : rows + N] = -sines
        inverse_z[v, 128 : 128 + N, rows + N : rows + 2 * N] = cosines
    fz = np.stack(halves(forward_z))
    iz = np.stack(halves(inverse_z))
    return forward_y, forward_x, inverse_x, inverse_y, fz, iz


def split(value):
    high = value.astype(BF16)
    return high, (value - high.astype(F32)).astype(BF16)


def mm(left, right):
    return jnp.dot(left, right, preferred_element_type=F32)


def apply_left(table, value):
    high, low = split(value)
    both = mm(table[...], high)
    return both[:192] + both[192:] + mm(table[0:192, :], low)


def apply_right(value, table, v):
    high, low = split(value)
    return mm(high, table[0, v]) + mm(low, table[0, v]) + mm(high, table[1, v])


def lanes(shape):
    return lax.broadcasted_iota(jnp.int32, shape, 1)


def depth_step(x_ref, x, fz, z_ref, slot):
    rows = jnp.concatenate([x_ref[x, :, 384 * u : 384 * u + 384] for u in range(48)], axis=0)
    for v in (0, 1):
        out = apply_right(rows[:, 128 * v : 128 * v + 256], fz, v)
        for part in (0, 1):
            z_ref[slot, x, 2 * v + part] = out[:, 128 * part : 128 * part + 128]


def rows_step(z_ref, fy, x, c, s_ref):
    sides = [
        jnp.concatenate([z_ref[f, x, i, pl.ds(c, 48, stride=8), :] for i in range(4)], axis=0)
        for f in (0, 1)
    ]
    out = apply_left(fy, jnp.concatenate(sides, axis=1))
    a_re, a_im = out[:96, :128], out[96:, :128]
    b_re, b_im = out[:96, 128:], out[96:, 128:]
    low = lanes((96, 128)) < 96
    packed = (
        jnp.where(low, a_re, pltpu.roll(b_im, 96, 1)),
        jnp.where(low, a_im, pltpu.roll(b_im, 64, 1)),
        jnp.where(low, b_re, pltpu.roll(b_im, 32, 1)),
    )
    for j in range(3):
        for q in range(3):
            s_ref[q, pl.ds((3 * j + x) * 8 + c, PEERS, stride=72), :] = packed[j][32 * q : 32 * q + 32]


def columns_step(r_ref, q, fx, c, h_ref):
    got = [
        jnp.concatenate(
            [r_ref[q, pl.ds((3 * j + x) * 8 + c, PEERS, stride=72), :] for x in range(3)], axis=0
        )
        for j in range(3)
    ]
    at = lanes((96, 128))
    b_im = jnp.where(
        at < 32, pltpu.roll(got[0], 32, 1), jnp.where(at < 64, pltpu.roll(got[1], 64, 1), pltpu.roll(got[2], 96, 1))
    )
    real = jnp.concatenate([got[0], got[2]], axis=1)
    imag = jnp.concatenate([got[1], b_im], axis=1)
    h_ref[c] = apply_left(fx, jnp.concatenate([real, imag], axis=0))


def contract_step(w_ref, h_ref, m_ref):
    @pl.loop(0, 12)
    def _(row):
        re = pl.ds(pl.multiple_of(row * 8, 8), 8)
        im = pl.ds(pl.multiple_of(row * 8 + 96, 8), 8)
        b_re = [h_ref[j, re, 128:] for j in range(8)]
        b_im = [h_ref[j, im, 128:] for j in range(8)]
        for ch in range(4):
            sum_re, sum_im = jnp.zeros((8, 128), F32), jnp.zeros((8, 128), F32)
            for i in range(8):
                mix_re = w_ref[ch * 64 + i * 8] * b_re[0]
                mix_im = w_ref[ch * 64 + i * 8] * b_im[0]
                for j in range(1, 8):
                    weight = w_ref[ch * 64 + i * 8 + j]
                    mix_re += weight * b_re[j]
                    mix_im += weight * b_im[j]
                a_re, a_im = h_ref[i, re, :128], h_ref[i, im, :128]
                sum_re += a_re * mix_re + a_im * mix_im
                sum_im += a_im * mix_re - a_re * mix_im
            m_ref[ch, re, :] = sum_re
            m_ref[ch, im, :] = sum_im


def columns_back_step(m_ref, ix, q, cs_ref):
    for pair in range(2):
        value = jnp.concatenate([m_ref[2 * pair], m_ref[2 * pair + 1]], axis=1)
        out = apply_left(ix, value)
        for k in range(2):
            ch = 2 * pair + k
            for part in range(2):
                for x in range(3):
                    at = 96 * part + 32 * x
                    cs_ref[q, pl.ds(8 * x + 4 * part + ch, PEERS, stride=24), :] = out[
                        at : at + 32, 128 * k : 128 * k + 128
                    ]


def rows_back_step(cr_ref, iy, x, pair, g_ref):
    sides = []
    for k in range(2):
        ch = 2 * pair + k
        sides.append(
            jnp.concatenate(
                [
                    cr_ref[q, pl.ds(8 * x + 4 * part + ch, PEERS, stride=24), :]
                    for part in range(2)
                    for q in range(3)
                ],
                axis=0,
            )
        )
    out = apply_left(iy, jnp.concatenate(sides, axis=1))
    for k in range(2):
        ch = 2 * pair + k
        for part in range(2):
            for v in range(2):
                at = 96 * part + 48 * v
                g_ref[x, 2 * v + part, pl.ds(ch, 48, stride=4), :] = out[at : at + 48, 128 * k : 128 * k + 128]


def depth_back_step(g_ref, iz, x, o_ref):
    outs = []
    for v in (0, 1):
        value = jnp.concatenate([g_ref[x, 2 * v], g_ref[x, 2 * v + 1]], axis=1)
        value = jnp.where(lax.rem(lanes((192, 256)), 128) < 96, value, 0.0)
        outs.append(apply_right(value, iz, v))
    o_ref[x, :, 0:128] = outs[0][:, :128]
    o_ref[x, :, 128:256] = outs[0][:, 128:] + outs[1][:, :128]
    o_ref[x, :, 256:384] = outs[1][:, 128:]


VMEM = pl.BlockSpec(memory_space=pltpu.VMEM)
SMEM = pl.BlockSpec(memory_space=pltpu.SMEM)
S_SHAPE = (3, PEERS * 72, 128)
C_SHAPE = (3, PEERS * 24, 128)
O_SHAPE = (3, 192, 384)


def params(**more):
    return pltpu.CompilerParams(vmem_limit_bytes=60_000_000, **more)


def forward_kernel(a_ref, b_ref, fz, fy, s_ref, z_ref):
    @pl.loop(0, 3)
    def _(x):
        depth_step(a_ref, x, fz, z_ref, 0)
        depth_step(b_ref, x, fz, z_ref, 1)

        @pl.loop(0, 8)
        def _(c):
            rows_step(z_ref, fy, x, c, s_ref)


def middle_kernel(w_ref, r_ref, fx, ix, cs_ref, h_ref, m_ref):
    @pl.loop(0, 3)
    def _(q):
        @pl.loop(0, 8)
        def _(c):
            columns_step(r_ref, q, fx, c, h_ref)

        contract_step(w_ref, h_ref, m_ref)
        columns_back_step(m_ref, ix, q, cs_ref)


def inverse_kernel(cr_ref, iy, iz, o_ref, g_ref):
    @pl.loop(0, 3)
    def _(x):
        for pair in range(2):
            rows_back_step(cr_ref, iy, x, pair, g_ref)
        depth_back_step(g_ref, iz, x, o_ref)


def exchange_kernel(rows, s_ref, r_ref, send_sem, recv_sem, own_sem):
    me, tm = lax.axis_index("space"), lax.axis_index("tm")
    barrier = pltpu.get_barrier_semaphore()
    for k in range(1, PEERS):
        pl.semaphore_signal(barrier, inc=1, device_id=(tm, lax.rem(me + k, PEERS)), device_id_type=MESH_ID)
    pl.semaphore_wait(barrier, PEERS - 1)
    mine = pl.ds(pl.multiple_of(me * rows, 8), rows)
    copies = []
    for k in range(1, PEERS):
        peer = lax.rem(me + k, PEERS)
        copy = pltpu.make_async_remote_copy(
            src_ref=s_ref.at[:, pl.ds(pl.multiple_of(peer * rows, 8), rows)],
            dst_ref=r_ref.at[:, mine],
            send_sem=send_sem.at[k],
            recv_sem=recv_sem.at[k],
            device_id=(tm, peer),
            device_id_type=MESH_ID,
        )
        copy.start()
        copies.append(copy)
    own = pltpu.make_async_copy(s_ref.at[:, mine], r_ref.at[:, mine], own_sem)
    own.start()
    own.wait()
    for copy in copies:
        copy.wait()


def times_kernel(o_ref, n_ref, send_sem, recv_sem):
    me, tm = lax.axis_index("space"), lax.axis_index("tm")
    barrier = pltpu.get_barrier_semaphore()
    near = (lax.rem(tm + 7, 8), lax.rem(tm + 1, 8))
    for k in range(2):
        pl.semaphore_signal(barrier, inc=1, device_id=(near[k], me), device_id_type=MESH_ID)
    pl.semaphore_wait(barrier, 2)
    copies = []
    for k in range(2):
        copy = pltpu.make_async_remote_copy(
            src_ref=o_ref,
            dst_ref=n_ref.at[k],
            send_sem=send_sem.at[k],
            recv_sem=recv_sem.at[k],
            device_id=(near[k], me),
            device_id_type=MESH_ID,
        )
        copy.start()
        copies.append(copy)
    for copy in copies:
        copy.wait()


def differences_kernel(o_ref, n_ref, c_ref, f_ref, d_ref):
    @pl.loop(0, 24)
    def _(pair):
        rows = pl.ds(pl.multiple_of(pair * 8, 8), 8)
        now, later, earlier = o_ref[0, rows, :], n_ref[0, 0, rows, :], n_ref[1, 0, rows, :]
        first = later - now
        second = later - 2.0 * now + earlier
        for half in range(2):
            out = pl.ds(pl.multiple_of(pair * 768 + half * 384, 128), 384)
            c_ref[0, :, out] = now[4 * half : 4 * half + 4]
            f_ref[0, :, out] = first[4 * half : 4 * half + 4]
            d_ref[0, :, out] = second[4 * half : 4 * half + 4]


def per_device(field_a, field_b, pairs, signs):
    components = field_a.shape[1]
    indices = jnp.arange(components, dtype=jnp.int32)
    first = (pairs[:, :, 0][:, :, None] == indices[None, None, :]).astype(F32)
    second = (pairs[:, :, 1][:, :, None] == indices[None, None, :]).astype(F32)
    weights = jnp.einsum("cp,cpi,cpj->cij", signs.astype(F32), first, second, precision=lax.Precision.HIGHEST)
    fy, fx, ix, iy, fz, iz = tables()
    a = jnp.transpose(field_a[0], (1, 0, 2))
    b = jnp.transpose(field_b[0], (1, 0, 2))
    sent = pl.pallas_call(
        forward_kernel,
        out_shape=jax.ShapeDtypeStruct(S_SHAPE, F32),
        in_specs=[VMEM] * 4,
        out_specs=VMEM,
        scratch_shapes=[pltpu.VMEM((2, 3, 4, 384, 128), F32)],
        compiler_params=params(),
        name="forward",
    )(a, b, fz, fy)

    def exchange(value, rows, number):
        return pl.pallas_call(
            functools.partial(exchange_kernel, rows),
            out_shape=jax.ShapeDtypeStruct(value.shape, F32),
            in_specs=[VMEM],
            out_specs=VMEM,
            scratch_shapes=[pltpu.SemaphoreType.DMA((PEERS,)), pltpu.SemaphoreType.DMA((PEERS,)), pltpu.SemaphoreType.DMA],
            compiler_params=params(collective_id=number, has_side_effects=True),
            name="exchange",
        )(value)

    received = exchange(sent, 72, 0)
    mixed = pl.pallas_call(
        middle_kernel,
        out_shape=jax.ShapeDtypeStruct(C_SHAPE, F32),
        in_specs=[SMEM] + [VMEM] * 3,
        out_specs=VMEM,
        scratch_shapes=[pltpu.VMEM((8, 192, 256), F32), pltpu.VMEM((4, 192, 128), F32)],
        compiler_params=params(),
        name="middle",
    )(weights.reshape(-1), received, fx, ix)
    returned = exchange(mixed, 24, 1)
    own = pl.pallas_call(
        inverse_kernel,
        out_shape=jax.ShapeDtypeStruct(O_SHAPE, F32),
        in_specs=[VMEM] * 3,
        out_specs=VMEM,
        scratch_shapes=[pltpu.VMEM((3, 4, 192, 128), F32)],
        compiler_params=params(),
        name="inverse",
    )(returned, iy, iz)
    near = pl.pallas_call(
        times_kernel,
        out_shape=jax.ShapeDtypeStruct((2,) + O_SHAPE, F32),
        in_specs=[VMEM],
        out_specs=VMEM,
        scratch_shapes=[pltpu.SemaphoreType.DMA((2,)), pltpu.SemaphoreType.DMA((2,))],
        compiler_params=params(collective_id=2, has_side_effects=True),
        name="times",
    )(own)
    block = pl.BlockSpec((1, 4, 18432), lambda x: (x, 0, 0))
    outs = pl.pallas_call(
        differences_kernel,
        grid=(3,),
        out_shape=[jax.ShapeDtypeStruct((3, 4, 18432), F32)] * 3,
        in_specs=[
            pl.BlockSpec((1, 192, 384), lambda x: (x, 0, 0)),
            pl.BlockSpec((2, 1, 192, 384), lambda x: (0, x, 0, 0)),
        ],
        out_specs=[block] * 3,
        compiler_params=params(),
        name="differences",
    )(own, near)
    return tuple(jnp.transpose(out, (1, 0, 2))[None] for out in outs)


def solution(mesh):
    spec = P("tm", None, "space", None)
    return jax.shard_map(
        per_device, mesh=mesh, in_specs=(spec, spec, P(), P()), out_specs=(spec,) * 3, check_vma=False
    )
```

time: 799 us -> 235 us (0.29)
  the two profiles are of different devices: /device:TPU:1 before, /device:TPU:94 now
where the time goes in v1:
time: 235 us; the launch traced here: 234 us
  Pallas kernels  231 us (98%)
    pallas_call x2, Pallas kernels, exchange(): pl.pallas_call(functools.partial(exchange_kernel, rows), out_shape=jax.Sh...  170 us
    pallas_call x1, Pallas kernels, per_device(): pl.pallas_call(middle_kernel, out_shape=jax.ShapeDtypeStruct(C_SHAPE, F32...  19.3 us
    pallas_call x1, Pallas kernels, per_device(): pl.pallas_call(times_kernel, out_shape=jax.ShapeDtypeStruct((2,) + O_SHAP...  18.8 us
    pallas_call x1, Pallas kernels, per_device(): pl.pallas_call(forward_kernel, out_shape=jax.ShapeDtypeStruct(S_SHAPE, F3...  14.6 us

profile of v1, /device:TPU:94, one launch (start us, length us, event | category | flops | bytes accessed | tf_op | source)
XLA Modules:
  0.0 234.3 jit_solution(10032141809882217040)
XLA Ops:
  0.6 0.7 convert_element_type.2
  1.3 0.8 fusion.7
  2.1 0.1 fusion
  2.2 0.7 reshape.9.w_ref
  2.9 14.6 %forward.1.s_ref = f32[3,2304,128]{2,1,0:T(8,128)} custom-call(f32[3,8,18432]{2,1,0:T(8,128)} %bitcast.17, f32[3,8,18432]{2,1,0:T(8,128)} %bitcast.18, bf16[2,2,256,256]{3,2,1,0:T(8,128)(2,1)} %constant.14.clone.fz, bf16[384,192]{1,0:T(8,128)(2,1)} %constant.15.clone.fy), custom_call_target="tpu_custom_call" | custom-call | tf_op jit(solution)/shard_map/forward/pallas_call | solution.py:323
  17.5 132.6 %exchange.2.r_ref = f32[3,2304,128]{2,1,0:T(8,128)} custom-call(f32[3,2304,128]{2,1,0:T(8,128)} %forward.1.s_ref), custom_call_target="tpu_custom_call" | custom-call | tf_op jit(solution)/shard_map/exchange/pallas_call | solution.py:334
  150.1 19.3 %middle.1.s_ref = f32[3,768,128]{2,1,0:T(8,128)} custom-call(f32[256]{0:T(256)} %reshape.9.w_ref, f32[3,2304,128]{2,1,0:T(8,128)} %exchange.2.r_ref, bf16[384,192]{1,0:T(8,128)(2,1)} %constant.16.clone.fx, bf16[384,192]{1,0:T(8,128)(2,1)} %constant.17.clone.ix), custom_call_target="tpu_custom_call" | custom-call | tf_op jit(solution)/shard_map/middle/pallas_call | solution.py:345
  169.4 37.5 %exchange.3.cr_ref = f32[3,768,128]{2,1,0:T(8,128)} custom-call(f32[3,768,128]{2,1,0:T(8,128)} %middle.1.s_ref), custom_call_target="tpu_custom_call" | custom-call | tf_op jit(solution)/shard_map/exchange/pallas_call | solution.py:334
  206.9 4.3 %inverse.1.o_ref = f32[3,192,384]{2,1,0:T(8,128)} custom-call(f32[3,768,128]{2,1,0:T(8,128)} %exchange.3.cr_ref, bf16[384,192]{1,0:T(8,128)(2,1)} %constant.18.clone.iy, bf16[2,2,256,256]{3,2,1,0:T(8,128)(2,1)} %constant.19.clone.iz), custom_call_target="tpu_custom_call" | custom-call | tf_op jit(solution)/shard_map/inverse/pallas_call | solution.py:355
  211.2 18.8 %times.1.n_ref = f32[2,3,192,384]{3,2,1,0:T(8,128)} custom-call(f32[3,192,384]{2,1,0:T(8,128)} %inverse.1.o_ref), custom_call_target="tpu_custom_call" | custom-call | tf_op jit(solution)/shard_map/times/pallas_call | solution.py:364
  230.0 4.3 %differences.1 = (f32[3,4,18432]{2,1,0:T(4,128)}, f32[3,4,18432]{2,1,0:T(4,128)}, f32[3,4,18432]{2,1,0:T(4,128)}) custom-call(f32[3,192,384]{2,1,0:T(8,128)} %inverse.1.o_ref, f32[2,3,192,384]{3,2,1,0:T(8,128)} %times.1.n_ref), custom_call_target="tpu_custom_call" | custom-call | tf_op jit(solution)/shard_map/differences/pallas_call | solution.py:374

commit v2 on v1

--- a/solution.py
+++ b/solution.py
@@ -1,4 +1,3 @@
-import functools
 import math
 
 import jax
@@ -116,13 +115,13 @@
     )
     for j in range(3):
         for q in range(3):
-            s_ref[q, pl.ds((3 * j + x) * 8 + c, PEERS, stride=72), :] = packed[j][32 * q : 32 * q + 32]
+            s_ref[q, pl.ds((3 * x + j) * 8 + c, PEERS, stride=72), :] = packed[j][32 * q : 32 * q + 32]
 
 
 def columns_step(r_ref, q, fx, c, h_ref):
     got = [
         jnp.concatenate(
-            [r_ref[q, pl.ds((3 * j + x) * 8 + c, PEERS, stride=72), :] for x in range(3)], axis=0
+            [r_ref[q, pl.ds((3 * x + j) * 8 + c, PEERS, stride=72), :] for x in range(3)], axis=0
         )
         for j in range(3)
     ]
@@ -208,107 +207,163 @@
 
 VMEM = pl.BlockSpec(memory_space=pltpu.VMEM)
 SMEM = pl.BlockSpec(memory_space=pltpu.SMEM)
-S_SHAPE = (3, PEERS * 72, 128)
-C_SHAPE = (3, PEERS * 24, 128)
-O_SHAPE = (3, 192, 384)
-
-
-def params(**more):
-    return pltpu.CompilerParams(vmem_limit_bytes=60_000_000, **more)
-
-
-def forward_kernel(a_ref, b_ref, fz, fy, s_ref, z_ref):
+ANY = pl.BlockSpec(memory_space=pl.ANY)
+
+
+def difference_step(o_ref, n_ref, out_ref, x):
+    for pair in range(24):
+        rows = pl.ds(pair * 8, 8)
+        now, later, earlier = o_ref[x, rows, :], n_ref[0, x, rows, :], n_ref[1, x, rows, :]
+        first = later - now
+        second = later - 2.0 * now + earlier
+        for half in range(2):
+            at = pl.ds(pair * 768 + half * 384, 384)
+            out_ref[0, x, :, at] = now[4 * half : 4 * half + 4]
+            out_ref[1, x, :, at] = first[4 * half : 4 * half + 4]
+            out_ref[2, x, :, at] = second[4 * half : 4 * half + 4]
+
+
+def whole_kernel(
+    a_hbm, b_hbm, w_ref, fz, fy, fx, ix, iy, iz,
+    c_hbm, f_hbm, d_hbm,
+    ab_ref, z_ref, s_ref, r_ref, h_ref, m_ref, cs_ref, cr_ref, g_ref, o_ref, n_ref, out_ref,
+    in_sem, out_sem, own_sem, fs_sem, fr_sem, cs_sem, cr_sem, ts_sem, tr_sem,
+):
+    me, tm = lax.axis_index("space"), lax.axis_index("tm")
+    near = (lax.rem(tm + 7, 8), lax.rem(tm + 1, 8))
+
+    def load(f, x):
+        return pltpu.make_async_copy((a_hbm, b_hbm)[f].at[x], ab_ref.at[f, x], in_sem.at[f, x])
+
+    for x in range(3):
+        for f in range(2):
+            load(f, x).start()
+    barrier = pltpu.get_barrier_semaphore()
+
+    @pl.loop(1, PEERS)
+    def _(k):
+        pl.semaphore_signal(barrier, inc=1, device_id=(tm, lax.rem(me + k, PEERS)), device_id_type=MESH_ID)
+
+    for k in range(2):
+        pl.semaphore_signal(barrier, inc=1, device_id=(near[k], me), device_id_type=MESH_ID)
+
+    def forward_copy(k, q, first, rows, part):
+        peer = lax.rem(me + k, PEERS)
+        return pltpu.make_async_remote_copy(
+            src_ref=s_ref.at[q, pl.ds(pl.multiple_of(peer * 72 + first, 8), rows)],
+            dst_ref=r_ref.at[q, pl.ds(pl.multiple_of(me * 72 + first, 8), rows)],
+            send_sem=fs_sem.at[part, k],
+            recv_sem=fr_sem.at[part, k],
+            device_id=(tm, peer),
+            device_id_type=MESH_ID,
+        )
+
+    def own_forward(q):
+        at = pl.ds(pl.multiple_of(me * 72, 8), 72)
+        return pltpu.make_async_copy(s_ref.at[q, at], r_ref.at[q, at], own_sem.at[q])
+
+    def back_copy(k, q):
+        peer = lax.rem(me + k, PEERS)
+        return pltpu.make_async_remote_copy(
+            src_ref=cs_ref.at[q, pl.ds(pl.multiple_of(peer * 24, 8), 24)],
+            dst_ref=cr_ref.at[q, pl.ds(pl.multiple_of(me * 24, 8), 24)],
+            send_sem=cs_sem.at[q, k],
+            recv_sem=cr_sem.at[q, k],
+            device_id=(tm, peer),
+            device_id_type=MESH_ID,
+        )
+
+    def own_back(q):
+        at = pl.ds(pl.multiple_of(me * 24, 8), 24)
+        return pltpu.make_async_copy(cs_ref.at[q, at], cr_ref.at[q, at], own_sem.at[3 + q])
+
+    def time_copy(k, x):
+        return pltpu.make_async_remote_copy(
+            src_ref=o_ref.at[x],
+            dst_ref=n_ref.at[k, x],
+            send_sem=ts_sem.at[k, x],
+            recv_sem=tr_sem.at[k, x],
+            device_id=(near[k], me),
+            device_id_type=MESH_ID,
+        )
+
+    def each_peer(act):
+        @pl.loop(1, PEERS)
+        def _(k):
+            act(k)
+
     @pl.loop(0, 3)
     def _(x):
-        depth_step(a_ref, x, fz, z_ref, 0)
-        depth_step(b_ref, x, fz, z_ref, 1)
+        for f in range(2):
+            load(f, x).wait()
+            depth_step(ab_ref.at[f], x, fz, z_ref, f)
 
         @pl.loop(0, 8)
         def _(c):
             rows_step(z_ref, fy, x, c, s_ref)
 
-
-def middle_kernel(w_ref, r_ref, fx, ix, cs_ref, h_ref, m_ref):
-    @pl.loop(0, 3)
-    def _(q):
+        @pl.when(x == 0)
+        def _():
+            pl.semaphore_wait(barrier, PEERS + 1)
+
+        each_peer(lambda k: forward_copy(k, 0, 24 * x, 24, x).start())
+
+    for q in (1, 2):
+        each_peer(lambda k: forward_copy(k, q, 0, 72, 2 + q).start())
+    for q in range(3):
+        own_forward(q).start()
+
+    for q in range(3):
+        own_forward(q).wait()
+        if q == 0:
+            for x in range(3):
+                each_peer(lambda k: forward_copy(k, 0, 24 * x, 24, x).wait_recv())
+        else:
+            each_peer(lambda k: forward_copy(k, q, 0, 72, 2 + q).wait_recv())
+
         @pl.loop(0, 8)
         def _(c):
             columns_step(r_ref, q, fx, c, h_ref)
 
         contract_step(w_ref, h_ref, m_ref)
         columns_back_step(m_ref, ix, q, cs_ref)
-
-
-def inverse_kernel(cr_ref, iy, iz, o_ref, g_ref):
+        each_peer(lambda k: back_copy(k, q).start())
+        own_back(q).start()
+
+    for q in range(3):
+        own_back(q).wait()
+        each_peer(lambda k: back_copy(k, q).wait_recv())
+
     @pl.loop(0, 3)
     def _(x):
         for pair in range(2):
             rows_back_step(cr_ref, iy, x, pair, g_ref)
         depth_back_step(g_ref, iz, x, o_ref)
-
-
-def exchange_kernel(rows, s_ref, r_ref, send_sem, recv_sem, own_sem):
-    me, tm = lax.axis_index("space"), lax.axis_index("tm")
-    barrier = pltpu.get_barrier_semaphore()
-    for k in range(1, PEERS):
-        pl.semaphore_signal(barrier, inc=1, device_id=(tm, lax.rem(me + k, PEERS)), device_id_type=MESH_ID)
-    pl.semaphore_wait(barrier, PEERS - 1)
-    mine = pl.ds(pl.multiple_of(me * rows, 8), rows)
-    copies = []
-    for k in range(1, PEERS):
-        peer = lax.rem(me + k, PEERS)
-        copy = pltpu.make_async_remote_copy(
-            src_ref=s_ref.at[:, pl.ds(pl.multiple_of(peer * rows, 8), rows)],
-            dst_ref=r_ref.at[:, mine],
-            send_sem=send_sem.at[k],
-            recv_sem=recv_sem.at[k],
-            device_id=(tm, peer),
-            device_id_type=MESH_ID,
-        )
-        copy.start()
-        copies.append(copy)
-    own = pltpu.make_async_copy(s_ref.at[:, mine], r_ref.at[:, mine], own_sem)
-    own.start()
-    own.wait()
-    for copy in copies:
-        copy.wait()
-
-
-def times_kernel(o_ref, n_ref, send_sem, recv_sem):
-    me, tm = lax.axis_index("space"), lax.axis_index("tm")
-    barrier = pltpu.get_barrier_semaphore()
-    near = (lax.rem(tm + 7, 8), lax.rem(tm + 1, 8))
-    for k in range(2):
-        pl.semaphore_signal(barrier, inc=1, device_id=(near[k], me), device_id_type=MESH_ID)
-    pl.semaphore_wait(barrier, 2)
-    copies = []
-    for k in range(2):
-        copy = pltpu.make_async_remote_copy(
-            src_ref=o_ref,
-            dst_ref=n_ref.at[k],
-            send_sem=send_sem.at[k],
-            recv_sem=recv_sem.at[k],
-            device_id=(near[k], me),
-            device_id_type=MESH_ID,
-        )
-        copy.start()
-        copies.append(copy)
-    for copy in copies:
-        copy.wait()
-
-
-def differences_kernel(o_ref, n_ref, c_ref, f_ref, d_ref):
-    @pl.loop(0, 24)
-    def _(pair):
-        rows = pl.ds(pl.multiple_of(pair * 8, 8), 8)
-        now, later, earlier = o_ref[0, rows, :], n_ref[0, 0, rows, :], n_ref[1, 0, rows, :]
-        first = later - now
-        second = later - 2.0 * now + earlier
-        for half in range(2):
-            out = pl.ds(pl.multiple_of(pair * 768 + half * 384, 128), 384)
-            c_ref[0, :, out] = now[4 * half : 4 * half + 4]
-            f_ref[0, :, out] = first[4 * half : 4 * half + 4]
-            d_ref[0, :, out] = second[4 * half : 4 * half + 4]
+        for k in range(2):
+            time_copy(k, x).start()
+
+    def store(i, x):
+        return pltpu.make_async_copy(out_ref.at[i, x], (c_hbm, f_hbm, d_hbm)[i].at[x], out_sem.at[i, x])
+
+    @pl.loop(0, 3)
+    def _(x):
+        for k in range(2):
+            time_copy(k, x).wait_recv()
+        difference_step(o_ref, n_ref, out_ref, x)
+        for i in range(3):
+            store(i, x).start()
+
+    for x in range(3):
+        each_peer(lambda k: forward_copy(k, 0, 24 * x, 24, x).wait_send())
+    for q in (1, 2):
+        each_peer(lambda k: forward_copy(k, q, 0, 72, 2 + q).wait_send())
+    for q in range(3):
+        each_peer(lambda k: back_copy(k, q).wait_send())
+    for x in range(3):
+        for k in range(2):
+            time_copy(k, x).wait_send()
+        for i in range(3):
+            store(i, x).wait()
 
 
 def per_device(field_a, field_b, pairs, signs):
@@ -320,69 +375,38 @@
     fy, fx, ix, iy, fz, iz = tables()
     a = jnp.transpose(field_a[0], (1, 0, 2))
     b = jnp.transpose(field_b[0], (1, 0, 2))
-    sent = pl.pallas_call(
-        forward_kernel,
-        out_shape=jax.ShapeDtypeStruct(S_SHAPE, F32),
-        in_specs=[VMEM] * 4,
-        out_specs=VMEM,
-        scratch_shapes=[pltpu.VMEM((2, 3, 4, 384, 128), F32)],
-        compiler_params=params(),
-        name="forward",
-    )(a, b, fz, fy)
-
-    def exchange(value, rows, number):
-        return pl.pallas_call(
-            functools.partial(exchange_kernel, rows),
-            out_shape=jax.ShapeDtypeStruct(value.shape, F32),
-            in_specs=[VMEM],
-            out_specs=VMEM,
-            scratch_shapes=[pltpu.SemaphoreType.DMA((PEERS,)), pltpu.SemaphoreType.DMA((PEERS,)), pltpu.SemaphoreType.DMA],
-            compiler_params=params(collective_id=number, has_side_effects=True),
-            name="exchange",
-        )(value)
-
-    received = exchange(sent, 72, 0)
-    mixed = pl.pallas_call(
-        middle_kernel,
-        out_shape=jax.ShapeDtypeStruct(C_SHAPE, F32),
-        in_specs=[SMEM] + [VMEM] * 3,
-        out_specs=VMEM,
-        scratch_shapes=[pltpu.VMEM((8, 192, 256), F32), pltpu.VMEM((4, 192, 128), F32)],
-        compiler_params=params(),
-        name="middle",
-    )(weights.reshape(-1), received, fx, ix)
-    returned = exchange(mixed, 24, 1)
-    own = pl.pallas_call(
-        inverse_kernel,
-        out_shape=jax.ShapeDtypeStruct(O_SHAPE, F32),
-        in_specs=[VMEM] * 3,
-        out_specs=VMEM,
-        scratch_shapes=[pltpu.VMEM((3, 4, 192, 128), F32)],
-        compiler_params=params(),
-        name="inverse",
-    )(returned, iy, iz)
-    near = pl.pallas_call(
-        times_kernel,
-        out_shape=jax.ShapeDtypeStruct((2,) + O_SHAPE, F32),
-        in_specs=[VMEM],
-        out_specs=VMEM,
-        scratch_shapes=[pltpu.SemaphoreType.DMA((2,)), pltpu.SemaphoreType.DMA((2,))],
-        compiler_params=params(collective_id=2, has_side_effects=True),
-        name="times",
-    )(own)
-    block = pl.BlockSpec((1, 4, 18432), lambda x: (x, 0, 0))
+    dma = pltpu.SemaphoreType.DMA
     outs = pl.pallas_call(
-        differences_kernel,
-        grid=(3,),
+        whole_kernel,
         out_shape=[jax.ShapeDtypeStruct((3, 4, 18432), F32)] * 3,
-        in_specs=[
-            pl.BlockSpec((1, 192, 384), lambda x: (x, 0, 0)),
-            pl.BlockSpec((2, 1, 192, 384), lambda x: (0, x, 0, 0)),
+        in_specs=[ANY, ANY, SMEM] + [VMEM] * 6,
+        out_specs=[ANY] * 3,
+        scratch_shapes=[
+            pltpu.VMEM((2, 3, 8, 18432), F32),
+            pltpu.VMEM((2, 3, 4, 384, 128), F32),
+            pltpu.VMEM((3, PEERS * 72, 128), F32),
+            pltpu.VMEM((3, PEERS * 72, 128), F32),
+            pltpu.VMEM((8, 192, 256), F32),
+            pltpu.VMEM((4, 192, 128), F32),
+            pltpu.VMEM((3, PEERS * 24, 128), F32),
+            pltpu.VMEM((3, PEERS * 24, 128), F32),
+            pltpu.VMEM((3, 4, 192, 128), F32),
+            pltpu.VMEM((3, 192, 384), F32),
+            pltpu.VMEM((2, 3, 192, 384), F32),
+            pltpu.VMEM((3, 3, 4, 18432), F32),
+            dma((2, 3)),
+            dma((3, 3)),
+            dma((6,)),
+            dma((5, PEERS)),
+            dma((5, PEERS)),
+            dma((3, PEERS)),
+            dma((3, PEERS)),
+            dma((2, 3)),
+            dma((2, 3)),
         ],
-        out_specs=[block] * 3,
-        compiler_params=params(),
-        name="differences",
-    )(own, near)
+        compiler_params=pltpu.CompilerParams(vmem_limit_bytes=60_000_000, collective_id=0, has_side_effects=True),
+        name="whole",
+    )(a, b, weights.reshape(-1), fz, fy, fx, ix, iy, iz)
     return tuple(jnp.transpose(out, (1, 0, 2))[None] for out in outs)
 
 

time: 235 us -> 155 us (0.66)
  the two profiles are of different devices: /device:TPU:94 before, /device:TPU:7 now
where the time goes in v2:
time: 155 us
  Pallas kernels  148 us (95%)
  local copies, waits for them, and re-layouts  5.52 us (4%)
    pallas_call x1, Pallas kernels, per_device(): pl.pallas_call(whole_kernel, out_shape=[jax.ShapeDtypeStruct((3, 4, 18432...  148 us
    unnamed x7, local copies, waits for them, and re-layouts  4.09 us

profile of v2, /device:TPU:7, one launch (start us, length us, event | category | flops | bytes accessed | tf_op | source)
XLA Modules:
  0.0 154.8 jit_solution(18436079197439658082)
XLA Ops:
  0.6 0.7 convert_element_type.2
  1.3 0.8 fusion.7
  2.1 0.1 fusion
  2.2 0.7 reshape.9.w_ref
  2.9 147.8 %whole.1 = (f32[3,4,18432]{2,1,0:T(4,128)}, f32[3,4,18432]{2,1,0:T(4,128)}, f32[3,4,18432]{2,1,0:T(4,128)}) custom-call(f32[3,8,18432]{2,1,0:T(8,128)} %bitcast.17, f32[3,8,18432]{2,1,0:T(8,128)} %bitcast.18, f32[256]{0:T(256)} %reshape.9.w_ref, bf16[2,2,256,256]{3,2,1,0:T(8,128)(2,1)} %constant.14.clone.fz, bf16[384,192]{1,0:T(8,128)(2,1)} %constant.15.clone.fy, ...), custom_call_target="tpu_custom_call" | custom-call | tf_op jit(solution)/shard_map/whole/pallas_call | solution.py:379
  150.7 0.0 copy-start.1
  150.7 0.0 copy-start
  150.7 2.3 %copy.16 = f32[1,4,3,18432]{3,1,2,0:T(4,128)} copy(f32[1,4,3,18432]{3,1,2,0:T(4,128)} %bitcast.21) | data formatting | bytes 1769472
  152.9 0.0 copy-done.1
  152.9 0.9 copy.17
  153.9 0.0 copy-done
  153.9 0.9 copy.18
Async XLA Ops:
  150.7 2.3 %copy-start.1 = (f32[3,4,18432]{2,1,0:T(4,128)S(1)}, f32[3,4,18432]{2,1,0:T(4,128)}, u32[]{:S(2)}) copy-start(f32[3,4,18432]{2,1,0:T(4,128)} %get-tuple-element.7) | copy-start | bytes 2654212
  150.7 3.2 %copy-start = (f32[3,4,18432]{2,1,0:T(4,128)S(1)}, f32[3,4,18432]{2,1,0:T(4,128)}, u32[]{:S(2)}) copy-start(f32[3,4,18432]{2,1,0:T(4,128)} %get-tuple-element.8) | copy-start | bytes 2654212

commit v3 on v2

--- a/solution.py
+++ b/solution.py
@@ -11,6 +11,7 @@
 
 N = 96
 PEERS = 32
+CELLS = 16
 MESH_ID = pl.DeviceIdType.MESH
 F32 = jnp.float32
 BF16 = jnp.bfloat16
@@ -115,13 +116,13 @@
     )
     for j in range(3):
         for q in range(3):
-            s_ref[q, pl.ds((3 * x + j) * 8 + c, PEERS, stride=72), :] = packed[j][32 * q : 32 * q + 32]
+            s_ref[q, x, pl.ds(8 * j + c, PEERS, stride=24), :] = packed[j][32 * q : 32 * q + 32]
 
 
 def columns_step(r_ref, q, fx, c, h_ref):
     got = [
         jnp.concatenate(
-            [r_ref[q, pl.ds((3 * x + j) * 8 + c, PEERS, stride=72), :] for x in range(3)], axis=0
+            [r_ref[q, x, pl.ds(8 * j + c, PEERS, stride=24), :] for x in range(3)], axis=0
         )
         for j in range(3)
     ]
@@ -134,6 +135,21 @@
     h_ref[c] = apply_left(fx, jnp.concatenate([real, imag], axis=0))
 
 
+def weights_step(pairs_ref, signs_ref, w_ref):
+    row = lax.broadcasted_iota(jnp.int32, (8, 128), 0)
+    lane = lax.broadcasted_iota(jnp.int32, (8, 128), 1)
+
+    @pl.loop(0, 4)
+    def _(ch):
+        total = jnp.zeros((8, 128), F32)
+        for p in range(16):
+            here = (row == pairs_ref[ch, 0, p]) & (lane == pairs_ref[ch, 1, p])
+            total += jnp.where(here, signs_ref[ch, p].astype(F32), 0.0)
+        for i in range(8):
+            for j in range(8):
+                w_ref[64 * ch + 8 * i + j] = jnp.broadcast_to(total[i : i + 1, j : j + 1], (8, 128))
+
+
 def contract_step(w_ref, h_ref, m_ref):
     @pl.loop(0, 12)
     def _(row):
@@ -141,11 +157,14 @@
         im = pl.ds(pl.multiple_of(row * 8 + 96, 8), 8)
         b_re = [h_ref[j, re, 128:] for j in range(8)]
         b_im = [h_ref[j, im, 128:] for j in range(8)]
-        for ch in range(4):
+
+        @pl.loop(0, 4)
+        def _(ch):
             sum_re, sum_im = jnp.zeros((8, 128), F32), jnp.zeros((8, 128), F32)
             for i in range(8):
-                mix_re = w_ref[ch * 64 + i * 8] * b_re[0]
-                mix_im = w_ref[ch * 64 + i * 8] * b_im[0]
+                weight = w_ref[ch * 64 + i * 8]
+                mix_re = weight * b_re[0]
+                mix_im = weight * b_im[0]
                 for j in range(1, 8):
                     weight = w_ref[ch * 64 + i * 8 + j]
                     mix_re += weight * b_re[j]
@@ -157,41 +176,65 @@
             m_ref[ch, im, :] = sum_im
 
 
-def columns_back_step(m_ref, ix, q, cs_ref):
+def columns_back_step(m_ref, ix, q, cs0_ref, cs_ref, k_ref):
+    at = lanes((32, 128))
     for pair in range(2):
         value = jnp.concatenate([m_ref[2 * pair], m_ref[2 * pair + 1]], axis=1)
         out = apply_left(ix, value)
-        for k in range(2):
-            ch = 2 * pair + k
-            for part in range(2):
-                for x in range(3):
-                    at = 96 * part + 32 * x
-                    cs_ref[q, pl.ds(8 * x + 4 * part + ch, PEERS, stride=24), :] = out[
-                        at : at + 32, 128 * k : 128 * k + 128
-                    ]
-
-
-def rows_back_step(cr_ref, iy, x, pair, g_ref):
+
+        def block(k, part, x):
+            first = 96 * part + 32 * x
+            return out[first : first + 32, 128 * k : 128 * k + 128]
+
+        @pl.when(q == 0)
+        def _():
+            for k in range(2):
+                for part in range(2):
+                    row = 4 * part + 2 * pair + k
+                    got = [block(k, part, x) for x in range(3)]
+                    for x in range(3):
+                        k_ref[0, 8 * x + row] = pltpu.roll(got[x], 96, 1)
+                        k_ref[1, 8 * x + row] = pltpu.roll(got[x], 64, 1)
+                    cs0_ref[pl.ds(row, PEERS, stride=8), :] = jnp.where(
+                        at < 32, pltpu.roll(got[0], 64, 1), jnp.where(at < 64, pltpu.roll(got[1], 96, 1), got[2])
+                    )
+
+        @pl.when(q > 0)
+        def _():
+            for k in range(2):
+                for part in range(2):
+                    for x in range(3):
+                        row = 8 * x + 4 * part + 2 * pair + k
+                        cs_ref[q - 1, pl.ds(row, PEERS, stride=24), :] = jnp.where(
+                            at < 96, block(k, part, x), k_ref[q - 1, row]
+                        )
+
+
+def rows_back_step(cr0_ref, cr_ref, iy, x, pair, g_ref):
+    at = lanes((32, 128))
     sides = []
     for k in range(2):
         ch = 2 * pair + k
-        sides.append(
-            jnp.concatenate(
-                [
-                    cr_ref[q, pl.ds(8 * x + 4 * part + ch, PEERS, stride=24), :]
-                    for part in range(2)
-                    for q in range(3)
-                ],
-                axis=0,
+        parts = []
+        for part in range(2):
+            own = cr0_ref[pl.ds(4 * part + ch, PEERS, stride=8), :]
+            second, third = (cr_ref[i, pl.ds(8 * x + 4 * part + ch, PEERS, stride=24), :] for i in range(2))
+            first = jnp.where(
+                at < 32,
+                pltpu.roll(second, 32, 1),
+                jnp.where(at < 64, pltpu.roll(third, 64, 1), pltpu.roll(own, (64 - 32 * x) % 128, 1)),
             )
-        )
+            parts += [first, second, third]
+        sides.append(jnp.concatenate(parts, axis=0))
     out = apply_left(iy, jnp.concatenate(sides, axis=1))
     for k in range(2):
         ch = 2 * pair + k
         for part in range(2):
             for v in range(2):
-                at = 96 * part + 48 * v
-                g_ref[x, 2 * v + part, pl.ds(ch, 48, stride=4), :] = out[at : at + 48, 128 * k : 128 * k + 128]
+                first = 96 * part + 48 * v
+                g_ref[x, 2 * v + part, pl.ds(ch, 48, stride=4), :] = out[
+                    first : first + 48, 128 * k : 128 * k + 128
+                ]
 
 
 def depth_back_step(g_ref, iz, x, o_ref):
@@ -224,13 +267,39 @@
 
 
 def whole_kernel(
-    a_hbm, b_hbm, w_ref, fz, fy, fx, ix, iy, iz,
+    a_hbm, b_hbm, pairs_ref, signs_ref, fz, fy, fx, ix, iy, iz,
     c_hbm, f_hbm, d_hbm,
-    ab_ref, z_ref, s_ref, r_ref, h_ref, m_ref, cs_ref, cr_ref, g_ref, o_ref, n_ref, out_ref,
-    in_sem, out_sem, own_sem, fs_sem, fr_sem, cs_sem, cr_sem, ts_sem, tr_sem,
+    ab_ref, z_ref, s_ref, t_ref, r_ref, h_ref, m_ref, w_ref, k_ref, cs0_ref, cs_ref, ct0_ref, ct_ref, cr0_ref, cr_ref, g_ref, o_ref, n_ref, out_ref,
+    in_sem, out_sem, own_sem, zs_sem, zr_sem, fs_sem, fr_sem, bs_sem, br_sem, cs_sem, cr_sem, ts_sem, tr_sem,
 ):
     me, tm = lax.axis_index("space"), lax.axis_index("tm")
     near = (lax.rem(tm + 7, 8), lax.rem(tm + 1, 8))
+    half, cell = me // CELLS, lax.rem(me, CELLS)
+    partner = lax.rem(me + CELLS, PEERS)
+    far = (1 - half) * CELLS
+
+    def cell_of(k):
+        along_x = lax.rem(cell // 4 + k // 4, 4)
+        along_y = lax.rem(lax.rem(cell, 4) + lax.rem(k, 4), 4)
+        return 4 * along_x + along_y
+
+    def rows(first, count=1):
+        return pl.ds(pl.multiple_of(first * 24, 8), count * 24)
+
+    def remote(src, dst, send, recv, space, time=None):
+        return pltpu.make_async_remote_copy(
+            src_ref=src,
+            dst_ref=dst,
+            send_sem=send,
+            recv_sem=recv,
+            device_id=(tm if time is None else time, space),
+            device_id_type=MESH_ID,
+        )
+
+    def each_cell(act):
+        @pl.loop(1, CELLS)
+        def _(k):
+            act(cell_of(k))
 
     def load(f, x):
         return pltpu.make_async_copy((a_hbm, b_hbm)[f].at[x], ab_ref.at[f, x], in_sem.at[f, x])
@@ -239,58 +308,72 @@
         for f in range(2):
             load(f, x).start()
     barrier = pltpu.get_barrier_semaphore()
-
-    @pl.loop(1, PEERS)
-    def _(k):
-        pl.semaphore_signal(barrier, inc=1, device_id=(tm, lax.rem(me + k, PEERS)), device_id_type=MESH_ID)
-
+    pl.semaphore_signal(barrier, inc=1, device_id=(tm, partner), device_id_type=MESH_ID)
+    each_cell(
+        lambda to: pl.semaphore_signal(
+            barrier, inc=1, device_id=(tm, half * CELLS + to), device_id_type=MESH_ID
+        )
+    )
     for k in range(2):
         pl.semaphore_signal(barrier, inc=1, device_id=(near[k], me), device_id_type=MESH_ID)
 
-    def forward_copy(k, q, first, rows, part):
-        peer = lax.rem(me + k, PEERS)
-        return pltpu.make_async_remote_copy(
-            src_ref=s_ref.at[q, pl.ds(pl.multiple_of(peer * 72 + first, 8), rows)],
-            dst_ref=r_ref.at[q, pl.ds(pl.multiple_of(me * 72 + first, 8), rows)],
-            send_sem=fs_sem.at[part, k],
-            recv_sem=fr_sem.at[part, k],
-            device_id=(tm, peer),
-            device_id_type=MESH_ID,
-        )
-
-    def own_forward(q):
-        at = pl.ds(pl.multiple_of(me * 72, 8), 72)
-        return pltpu.make_async_copy(s_ref.at[q, at], r_ref.at[q, at], own_sem.at[q])
-
-    def back_copy(k, q):
-        peer = lax.rem(me + k, PEERS)
-        return pltpu.make_async_remote_copy(
-            src_ref=cs_ref.at[q, pl.ds(pl.multiple_of(peer * 24, 8), 24)],
-            dst_ref=cr_ref.at[q, pl.ds(pl.multiple_of(me * 24, 8), 24)],
-            send_sem=cs_sem.at[q, k],
-            recv_sem=cr_sem.at[q, k],
-            device_id=(tm, peer),
-            device_id_type=MESH_ID,
-        )
-
-    def own_back(q):
-        at = pl.ds(pl.multiple_of(me * 24, 8), 24)
-        return pltpu.make_async_copy(cs_ref.at[q, at], cr_ref.at[q, at], own_sem.at[3 + q])
+    def cross(q, x):
+        return remote(s_ref.at[q, x, rows(far, CELLS)], t_ref.at[q, x], zs_sem.at[q, x], zr_sem.at[q, x], partner)
+
+    def spread(q, x, to):
+        at = half * CELLS + to
+        return remote(s_ref.at[q, x, rows(at)], r_ref.at[q, x, rows(me)], fs_sem.at[0], fr_sem.at[0, q], at)
+
+    def relay(q, x, to):
+        at = half * CELLS + to
+        return remote(t_ref.at[q, x, rows(to)], r_ref.at[q, x, rows(partner)], fs_sem.at[1], fr_sem.at[1, q], at)
+
+    def keep(q, x):
+        return pltpu.make_async_copy(s_ref.at[q, x, rows(me)], r_ref.at[q, x, rows(me)], own_sem.at[0, q, x])
+
+    def keep_relay(q, x):
+        return pltpu.make_async_copy(t_ref.at[q, x, rows(cell)], r_ref.at[q, x, rows(partner)], own_sem.at[1, q, x])
+
+    def group(refs, g, first, count=1):
+        size = 24 if g else 8
+        at = pl.ds(pl.multiple_of(first * size, 8), count * size)
+        return refs[1].at[g - 1, at] if g else refs[0].at[at]
+
+    made, passed, final = (cs0_ref, cs_ref), (ct0_ref, ct_ref), (cr0_ref, cr_ref)
+
+    def cross_back(g):
+        return remote(group(made, g, far, CELLS), group(passed, g, 0, CELLS), bs_sem.at[g], br_sem.at[g], partner)
+
+    def spread_back(g, to):
+        at = half * CELLS + to
+        return remote(group(made, g, at), group(final, g, me), cs_sem.at[0, g], cr_sem.at[0, g], at)
+
+    def relay_back(g, to):
+        at = half * CELLS + to
+        return remote(group(passed, g, to), group(final, g, partner), cs_sem.at[1, g], cr_sem.at[1, g], at)
+
+    def all_back(i, g):
+        some = group(final, g, 0, CELLS - 1)
+        return remote(some, some, cs_sem.at[i, g], cr_sem.at[i, g], partner)
+
+    def keep_back(g):
+        return pltpu.make_async_copy(group(made, g, me), group(final, g, me), own_sem.at[2, g, 0])
+
+    def keep_relay_back(g):
+        return pltpu.make_async_copy(group(passed, g, cell), group(final, g, partner), own_sem.at[2, g, 1])
+
+    def send_back(g):
+        cross_back(g).start()
+        each_cell(lambda to: spread_back(g, to).start())
+        keep_back(g).start()
 
     def time_copy(k, x):
-        return pltpu.make_async_remote_copy(
-            src_ref=o_ref.at[x],
-            dst_ref=n_ref.at[k, x],
-            send_sem=ts_sem.at[k, x],
-            recv_sem=tr_sem.at[k, x],
-            device_id=(near[k], me),
-            device_id_type=MESH_ID,
-        )
-
-    def each_peer(act):
-        @pl.loop(1, PEERS)
-        def _(k):
-            act(k)
+        return remote(o_ref.at[x], n_ref.at[k, x], ts_sem.at[k, x], tr_sem.at[k, x], me, near[k])
+
+    def send(q, x):
+        cross(q, x).start()
+        each_cell(lambda to: spread(q, x, to).start())
+        keep(q, x).start()
 
     @pl.loop(0, 3)
     def _(x):
@@ -304,40 +387,58 @@
 
         @pl.when(x == 0)
         def _():
-            pl.semaphore_wait(barrier, PEERS + 1)
-
-        each_peer(lambda k: forward_copy(k, 0, 24 * x, 24, x).start())
-
-    for q in (1, 2):
-        each_peer(lambda k: forward_copy(k, q, 0, 72, 2 + q).start())
-    for q in range(3):
-        own_forward(q).start()
-
-    for q in range(3):
-        own_forward(q).wait()
-        if q == 0:
-            for x in range(3):
-                each_peer(lambda k: forward_copy(k, 0, 24 * x, 24, x).wait_recv())
-        else:
-            each_peer(lambda k: forward_copy(k, q, 0, 72, 2 + q).wait_recv())
+            pl.semaphore_wait(barrier, CELLS + 2)
+
+        send(0, x)
+
+    @pl.loop(0, 6)
+    def _(i):
+        send(1 + i // 3, lax.rem(i, 3))
+
+    every = pl.ds(0, 24 * (CELLS - 1))
+    weights_step(pairs_ref, signs_ref, w_ref)
+
+    @pl.loop(0, 3)
+    def _(q):
+        @pl.loop(0, 3)
+        def _(x):
+            cross(q, x).wait_recv()
+            each_cell(lambda to: relay(q, x, to).start())
+            keep_relay(q, x).start()
+            keep(q, x).wait()
+
+        for i in range(2):
+            remote(r_ref.at[q, :, every], r_ref.at[q, :, every], fs_sem.at[i], fr_sem.at[i, q], partner).wait_recv()
+
+        @pl.loop(0, 3)
+        def _(x):
+            keep_relay(q, x).wait()
 
         @pl.loop(0, 8)
         def _(c):
             columns_step(r_ref, q, fx, c, h_ref)
 
         contract_step(w_ref, h_ref, m_ref)
-        columns_back_step(m_ref, ix, q, cs_ref)
-        each_peer(lambda k: back_copy(k, q).start())
-        own_back(q).start()
-
-    for q in range(3):
-        own_back(q).wait()
-        each_peer(lambda k: back_copy(k, q).wait_recv())
-
-    @pl.loop(0, 3)
-    def _(x):
+        columns_back_step(m_ref, ix, q, cs0_ref, cs_ref, k_ref)
+        for g in range(3):
+
+            @pl.when(q == g)
+            def _():
+                send_back(g)
+
+    for g in range(3):
+        cross_back(g).wait_recv()
+        each_cell(lambda to: relay_back(g, to).start())
+        keep_relay_back(g).start()
+        keep_back(g).wait()
+    for g in range(3):
+        for i in range(2):
+            all_back(i, g).wait_recv()
+        keep_relay_back(g).wait()
+
+    for x in range(3):
         for pair in range(2):
-            rows_back_step(cr_ref, iy, x, pair, g_ref)
+            rows_back_step(cr0_ref, cr_ref, iy, x, pair, g_ref)
         depth_back_step(g_ref, iz, x, o_ref)
         for k in range(2):
             time_copy(k, x).start()
@@ -353,25 +454,24 @@
         for i in range(3):
             store(i, x).start()
 
-    for x in range(3):
-        each_peer(lambda k: forward_copy(k, 0, 24 * x, 24, x).wait_send())
-    for q in (1, 2):
-        each_peer(lambda k: forward_copy(k, q, 0, 72, 2 + q).wait_send())
-    for q in range(3):
-        each_peer(lambda k: back_copy(k, q).wait_send())
-    for x in range(3):
+    for i in range(2):
+        remote(s_ref.at[:, :, every], s_ref.at[:, :, every], fs_sem.at[i], fr_sem.at[i, 0], partner).wait_send()
+        for g in range(3):
+            all_back(i, g).wait_send()
+    for g in range(3):
+        cross_back(g).wait_send()
+
+    @pl.loop(0, 3)
+    def _(q):
+        for x in range(3):
+            cross(q, x).wait_send()
         for k in range(2):
-            time_copy(k, x).wait_send()
+            time_copy(k, q).wait_send()
         for i in range(3):
-            store(i, x).wait()
+            store(i, q).wait()
 
 
 def per_device(field_a, field_b, pairs, signs):
-    components = field_a.shape[1]
-    indices = jnp.arange(components, dtype=jnp.int32)
-    first = (pairs[:, :, 0][:, :, None] == indices[None, None, :]).astype(F32)
-    second = (pairs[:, :, 1][:, :, None] == indices[None, None, :]).astype(F32)
-    weights = jnp.einsum("cp,cpi,cpj->cij", signs.astype(F32), first, second, precision=lax.Precision.HIGHEST)
     fy, fx, ix, iy, fz, iz = tables()
     a = jnp.transpose(field_a[0], (1, 0, 2))
     b = jnp.transpose(field_b[0], (1, 0, 2))
@@ -379,34 +479,45 @@
     outs = pl.pallas_call(
         whole_kernel,
         out_shape=[jax.ShapeDtypeStruct((3, 4, 18432), F32)] * 3,
-        in_specs=[ANY, ANY, SMEM] + [VMEM] * 6,
+        in_specs=[ANY, ANY, SMEM, SMEM] + [VMEM] * 6,
         out_specs=[ANY] * 3,
         scratch_shapes=[
             pltpu.VMEM((2, 3, 8, 18432), F32),
             pltpu.VMEM((2, 3, 4, 384, 128), F32),
-            pltpu.VMEM((3, PEERS * 72, 128), F32),
-            pltpu.VMEM((3, PEERS * 72, 128), F32),
+            pltpu.VMEM((3, 3, PEERS * 24, 128), F32),
+            pltpu.VMEM((3, 3, CELLS * 24, 128), F32),
+            pltpu.VMEM((3, 3, PEERS * 24, 128), F32),
             pltpu.VMEM((8, 192, 256), F32),
             pltpu.VMEM((4, 192, 128), F32),
-            pltpu.VMEM((3, PEERS * 24, 128), F32),
-            pltpu.VMEM((3, PEERS * 24, 128), F32),
+            pltpu.VMEM((256, 8, 128), F32),
+            pltpu.VMEM((2, 24, PEERS, 128), F32),
+            pltpu.VMEM((PEERS * 8, 128), F32),
+            pltpu.VMEM((2, PEERS * 24, 128), F32),
+            pltpu.VMEM((CELLS * 8, 128), F32),
+            pltpu.VMEM((2, CELLS * 24, 128), F32),
+            pltpu.VMEM((PEERS * 8, 128), F32),
+            pltpu.VMEM((2, PEERS * 24, 128), F32),
             pltpu.VMEM((3, 4, 192, 128), F32),
             pltpu.VMEM((3, 192, 384), F32),
             pltpu.VMEM((2, 3, 192, 384), F32),
             pltpu.VMEM((3, 3, 4, 18432), F32),
             dma((2, 3)),
             dma((3, 3)),
-            dma((6,)),
-            dma((5, PEERS)),
-            dma((5, PEERS)),
-            dma((3, PEERS)),
-            dma((3, PEERS)),
+            dma((3, 3, 3)),
+            dma((3, 3)),
+            dma((3, 3)),
+            dma((2,)),
+            dma((2, 3)),
+            dma((3,)),
+            dma((3,)),
+            dma((2, 3)),
+            dma((2, 3)),
             dma((2, 3)),
             dma((2, 3)),
         ],
         compiler_params=pltpu.CompilerParams(vmem_limit_bytes=60_000_000, collective_id=0, has_side_effects=True),
         name="whole",
-    )(a, b, weights.reshape(-1), fz, fy, fx, ix, iy, iz)
+    )(a, b, jnp.transpose(pairs, (0, 2, 1)), signs, fz, fy, fx, ix, iy, iz)
     return tuple(jnp.transpose(out, (1, 0, 2))[None] for out in outs)
 
 

time: 155 us -> 146 us (0.942)
  the two profiles are of different devices: /device:TPU:7 before, /device:TPU:1 now
where the time goes in v3:
time: 146 us
  Pallas kernels  141 us (97%)
  local copies, waits for them, and re-layouts  4.09 us (3%)
    pallas_call x1, Pallas kernels, per_device(): pl.pallas_call(whole_kernel, out_shape=[jax.ShapeDtypeStruct((3, 4, 18432...  141 us
    unnamed x7, local copies, waits for them, and re-layouts  4.09 us

profile of v3, /device:TPU:1, one launch (start us, length us, event | category | flops | bytes accessed | tf_op | source)
XLA Modules:
  0.0 145.6 jit_solution(17742725528897304232)
XLA Ops:
  0.6 140.9 %whole.1 = (f32[3,4,18432]{2,1,0:T(4,128)}, f32[3,4,18432]{2,1,0:T(4,128)}, f32[3,4,18432]{2,1,0:T(4,128)}) custom-call(f32[3,8,18432]{2,1,0:T(8,128)} %bitcast.16, f32[3,8,18432]{2,1,0:T(8,128)} %bitcast.17, s32[4,2,16]{2,1,0:T(2,128)} %bitcast.21, s32[4,16]{1,0:T(4,128)} %signs_ref.1, bf16[2,2,256,256]{3,2,1,0:T(8,128)(2,1)} %constant.12.clone.fz, ...), custom_call_target="tpu_custom_call" | custom-call | tf_op jit(solution)/shard_map/whole/pallas_call | solution.py:479
  141.5 0.0 copy-start.1
  141.5 0.0 copy-start
  141.5 2.3 %copy.16 = f32[1,4,3,18432]{3,1,2,0:T(4,128)} copy(f32[1,4,3,18432]{3,1,2,0:T(4,128)} %bitcast.20) | data formatting | bytes 1769472
  143.8 0.0 copy-done.1
  143.8 0.9 copy.17
  144.7 0.0 copy-done
  144.7 0.9 copy.18
Async XLA Ops:
  141.5 2.3 %copy-start.1 = (f32[3,4,18432]{2,1,0:T(4,128)S(1)}, f32[3,4,18432]{2,1,0:T(4,128)}, u32[]{:S(2)}) copy-start(f32[3,4,18432]{2,1,0:T(4,128)} %get-tuple-element.7) | copy-start | bytes 2654212
  141.5 3.2 %copy-start = (f32[3,4,18432]{2,1,0:T(4,128)S(1)}, f32[3,4,18432]{2,1,0:T(4,128)}, u32[]{:S(2)}) copy-start(f32[3,4,18432]{2,1,0:T(4,128)} %get-tuple-element.8) | copy-start | bytes 2654212

commit v4 on v3

--- a/solution.py
+++ b/solution.py
@@ -266,10 +266,38 @@
             out_ref[2, x, :, at] = second[4 * half : 4 * half + 4]
 
 
+def differences_kernel(o_hbm, n_hbm, c_hbm, f_hbm, d_hbm, o_ref, n_ref, out_ref, in_sem, out_sem):
+    def loads(x):
+        return (
+            pltpu.make_async_copy(o_hbm.at[x], o_ref.at[x], in_sem.at[0, x]),
+            pltpu.make_async_copy(n_hbm.at[0, x], n_ref.at[0, x], in_sem.at[1, x]),
+            pltpu.make_async_copy(n_hbm.at[1, x], n_ref.at[1, x], in_sem.at[2, x]),
+        )
+
+    def store(i, x):
+        return pltpu.make_async_copy(out_ref.at[i, x], (c_hbm, f_hbm, d_hbm)[i].at[x], out_sem.at[i, x])
+
+    for x in range(3):
+        for copy in loads(x):
+            copy.start()
+
+    @pl.loop(0, 3)
+    def _(x):
+        for copy in loads(x):
+            copy.wait()
+        difference_step(o_ref, n_ref, out_ref, x)
+        for i in range(3):
+            store(i, x).start()
+
+    for x in range(3):
+        for i in range(3):
+            store(i, x).wait()
+
+
 def whole_kernel(
     a_hbm, b_hbm, pairs_ref, signs_ref, fz, fy, fx, ix, iy, iz,
-    c_hbm, f_hbm, d_hbm,
-    ab_ref, z_ref, s_ref, t_ref, r_ref, h_ref, m_ref, w_ref, k_ref, cs0_ref, cs_ref, ct0_ref, ct_ref, cr0_ref, cr_ref, g_ref, o_ref, n_ref, out_ref,
+    o_hbm, n_hbm,
+    ab_ref, z_ref, s_ref, t_ref, r_ref, h_ref, m_ref, w_ref, k_ref, cs0_ref, cs_ref, ct0_ref, ct_ref, cr0_ref, cr_ref, g_ref, o_ref,
     in_sem, out_sem, own_sem, zs_sem, zr_sem, fs_sem, fr_sem, bs_sem, br_sem, cs_sem, cr_sem, ts_sem, tr_sem,
 ):
     me, tm = lax.axis_index("space"), lax.axis_index("tm")
@@ -368,7 +396,10 @@
         keep_back(g).start()
 
     def time_copy(k, x):
-        return remote(o_ref.at[x], n_ref.at[k, x], ts_sem.at[k, x], tr_sem.at[k, x], me, near[k])
+        return remote(o_ref.at[x], n_hbm.at[k, x], ts_sem.at[k, x], tr_sem.at[k, x], me, near[k])
+
+    def store(x):
+        return pltpu.make_async_copy(o_ref.at[x], o_hbm.at[x], out_sem.at[x])
 
     def send(q, x):
         cross(q, x).start()
@@ -381,7 +412,7 @@
             load(f, x).wait()
             depth_step(ab_ref.at[f], x, fz, z_ref, f)
 
-        @pl.loop(0, 8)
+        @pl.loop(0, 8, unroll=4)
         def _(c):
             rows_step(z_ref, fy, x, c, s_ref)
 
@@ -414,7 +445,7 @@
         def _(x):
             keep_relay(q, x).wait()
 
-        @pl.loop(0, 8)
+        @pl.loop(0, 8, unroll=4)
         def _(c):
             columns_step(r_ref, q, fx, c, h_ref)
 
@@ -442,17 +473,7 @@
         depth_back_step(g_ref, iz, x, o_ref)
         for k in range(2):
             time_copy(k, x).start()
-
-    def store(i, x):
-        return pltpu.make_async_copy(out_ref.at[i, x], (c_hbm, f_hbm, d_hbm)[i].at[x], out_sem.at[i, x])
-
-    @pl.loop(0, 3)
-    def _(x):
-        for k in range(2):
-            time_copy(k, x).wait_recv()
-        difference_step(o_ref, n_ref, out_ref, x)
-        for i in range(3):
-            store(i, x).start()
+        store(x).start()
 
     for i in range(2):
         remote(s_ref.at[:, :, every], s_ref.at[:, :, every], fs_sem.at[i], fr_sem.at[i, 0], partner).wait_send()
@@ -467,8 +488,8 @@
             cross(q, x).wait_send()
         for k in range(2):
             time_copy(k, q).wait_send()
-        for i in range(3):
-            store(i, q).wait()
+            time_copy(k, q).wait_recv()
+        store(q).wait()
 
 
 def per_device(field_a, field_b, pairs, signs):
@@ -476,11 +497,11 @@
     a = jnp.transpose(field_a[0], (1, 0, 2))
     b = jnp.transpose(field_b[0], (1, 0, 2))
     dma = pltpu.SemaphoreType.DMA
-    outs = pl.pallas_call(
+    own, others = pl.pallas_call(
         whole_kernel,
-        out_shape=[jax.ShapeDtypeStruct((3, 4, 18432), F32)] * 3,
+        out_shape=[jax.ShapeDtypeStruct((3, 192, 384), F32), jax.ShapeDtypeStruct((2, 3, 192, 384), F32)],
         in_specs=[ANY, ANY, SMEM, SMEM] + [VMEM] * 6,
-        out_specs=[ANY] * 3,
+        out_specs=[ANY] * 2,
         scratch_shapes=[
             pltpu.VMEM((2, 3, 8, 18432), F32),
             pltpu.VMEM((2, 3, 4, 384, 128), F32),
@@ -499,10 +520,8 @@
             pltpu.VMEM((2, PEERS * 24, 128), F32),
             pltpu.VMEM((3, 4, 192, 128), F32),
             pltpu.VMEM((3, 192, 384), F32),
-            pltpu.VMEM((2, 3, 192, 384), F32),
-            pltpu.VMEM((3, 3, 4, 18432), F32),
             dma((2, 3)),
-            dma((3, 3)),
+            dma((3,)),
             dma((3, 3, 3)),
             dma((3, 3)),
             dma((3, 3)),
@@ -518,6 +537,21 @@
         compiler_params=pltpu.CompilerParams(vmem_limit_bytes=60_000_000, collective_id=0, has_side_effects=True),
         name="whole",
     )(a, b, jnp.transpose(pairs, (0, 2, 1)), signs, fz, fy, fx, ix, iy, iz)
+    outs = pl.pallas_call(
+        differences_kernel,
+        out_shape=[jax.ShapeDtypeStruct((3, 4, 18432), F32)] * 3,
+        in_specs=[ANY] * 2,
+        out_specs=[ANY] * 3,
+        scratch_shapes=[
+            pltpu.VMEM((3, 192, 384), F32),
+            pltpu.VMEM((2, 3, 192, 384), F32),
+            pltpu.VMEM((3, 3, 4, 18432), F32),
+            dma((3, 3)),
+            dma((3, 3)),
+        ],
+        compiler_params=pltpu.CompilerParams(vmem_limit_bytes=62_000_000),
+        name="differences",
+    )(own, others)
     return tuple(jnp.transpose(out, (1, 0, 2))[None] for out in outs)
 
 

time: 146 us -> 141 us (0.966)
  local copies, waits for them, and re-layouts: 4.09 us -> 0 us
    unnamed x7 -> x0, local copies, waits for them, and re-layouts: 4.09 us -> none
    pallas_call x1 -> x2, Pallas kernels: 141 us -> 141 us  [the longest x1 138 us: per_device(): pl.pallas_call(whole_kernel, out_shape=[jax.ShapeDtypeStruct((3, 192, 384...]
where the time goes in v4:
time: 141 us
  Pallas kernels  141 us (100%)
    pallas_call x1, Pallas kernels, per_device(): pl.pallas_call(whole_kernel, out_shape=[jax.ShapeDtypeStruct((3, 192, 384...  138 us
    pallas_call x1, Pallas kernels, per_device(): pl.pallas_call(differences_kernel, out_shape=[jax.ShapeDtypeStruct((3, 4,...  2.87 us

profile of v4, /device:TPU:1, one launch (start us, length us, event | category | flops | bytes accessed | tf_op | source)
XLA Modules:
  0.0 141.2 jit_solution(14014320913125998317)
XLA Ops:
  0.6 137.7 %whole.1 = (f32[3,192,384]{2,1,0:T(8,128)}, f32[2,3,192,384]{3,2,1,0:T(8,128)}) custom-call(f32[3,8,18432]{2,1,0:T(8,128)} %bitcast.16, f32[3,8,18432]{2,1,0:T(8,128)} %bitcast.17, s32[4,2,16]{2,1,0:T(2,128)} %bitcast.18, s32[4,16]{1,0:T(4,128)} %signs_ref.1, bf16[2,2,256,256]{3,2,1,0:T(8,128)(2,1)} %constant.12.clone.fz, ...), custom_call_target="tpu_custom_call" | custom-call | tf_op jit(solution)/shard_map/whole/pallas_call | solution.py:500
  138.3 2.9 %differences.1 = (f32[3,4,18432]{2,1,0:T(4,128)}, f32[3,4,18432]{2,1,0:T(4,128)}, f32[3,4,18432]{2,1,0:T(4,128)}) custom-call(f32[3,192,384]{2,1,0:T(8,128)} %get-tuple-element.8.o_hbm, f32[2,3,192,384]{3,2,1,0:T(8,128)} %get-tuple-element.9.n_hbm), custom_call_target="tpu_custom_call" | custom-call | tf_op jit(solution)/shard_map/differences/pallas_call | solution.py:540

commit v5 on v4

--- a/solution.py
+++ b/solution.py
@@ -295,16 +295,18 @@
 
 
 def whole_kernel(
-    a_hbm, b_hbm, pairs_ref, signs_ref, fz, fy, fx, ix, iy, iz,
+    a_hbm, b_hbm, pairs_ref, signs_ref, fz_hbm, fy_hbm, fx_hbm, ix_hbm, iy_hbm, iz_hbm,
     o_hbm, n_hbm,
-    ab_ref, z_ref, s_ref, t_ref, r_ref, h_ref, m_ref, w_ref, k_ref, cs0_ref, cs_ref, ct0_ref, ct_ref, cr0_ref, cr_ref, g_ref, o_ref,
-    in_sem, out_sem, own_sem, zs_sem, zr_sem, fs_sem, fr_sem, bs_sem, br_sem, cs_sem, cr_sem, ts_sem, tr_sem,
+    ab_ref, z_ref, s_ref, t_ref, r_ref, h_ref, m_ref, w_ref, k_ref, cs0_ref, cs_ref, ct0_ref, ct_ref, cr0_ref, cr_ref, et0_ref, et_ref, ef0_ref, ef_ref, g_ref, o_ref, e_ref, fz, fy, fx, ix, iy, iz,
+    table_sem, in_sem, out_sem, own_sem, zs_sem, zr_sem, fs_sem, fr_sem, bs_sem, br_sem, cs_sem, cr_sem, ts_sem, tr_sem, es_sem, er_sem, fs2_sem, fr2_sem, ek_sem,
 ):
     me, tm = lax.axis_index("space"), lax.axis_index("tm")
     near = (lax.rem(tm + 7, 8), lax.rem(tm + 1, 8))
     half, cell = me // CELLS, lax.rem(me, CELLS)
     partner = lax.rem(me + CELLS, PEERS)
     far = (1 - half) * CELLS
+    at_end = lax.rem(tm, 7) == 0
+    other = 7 - tm
 
     def cell_of(k):
         along_x = lax.rem(cell // 4 + k // 4, 4)
@@ -332,9 +334,20 @@
     def load(f, x):
         return pltpu.make_async_copy((a_hbm, b_hbm)[f].at[x], ab_ref.at[f, x], in_sem.at[f, x])
 
-    for x in range(3):
+    tables_hbm = (fz_hbm, fy_hbm, fx_hbm, ix_hbm, iy_hbm, iz_hbm)
+    loads = [
+        pltpu.make_async_copy(src, dst, table_sem.at[i])
+        for i, (src, dst) in enumerate(zip(tables_hbm, (fz, fy, fx, ix, iy, iz)))
+    ]
+    for f in range(2):
+        load(f, 0).start()
+    for copy in loads[:2]:
+        copy.start()
+    for x in range(1, 3):
         for f in range(2):
             load(f, x).start()
+    for copy in loads[2:]:
+        copy.start()
     barrier = pltpu.get_barrier_semaphore()
     pl.semaphore_signal(barrier, inc=1, device_id=(tm, partner), device_id_type=MESH_ID)
     each_cell(
@@ -345,6 +358,10 @@
     for k in range(2):
         pl.semaphore_signal(barrier, inc=1, device_id=(near[k], me), device_id_type=MESH_ID)
 
+    @pl.when(at_end)
+    def _():
+        pl.semaphore_signal(barrier, inc=1, device_id=(other, partner), device_id_type=MESH_ID)
+
     def cross(q, x):
         return remote(s_ref.at[q, x, rows(far, CELLS)], t_ref.at[q, x], zs_sem.at[q, x], zr_sem.at[q, x], partner)
 
@@ -390,6 +407,29 @@
     def keep_relay_back(g):
         return pltpu.make_async_copy(group(passed, g, cell), group(final, g, partner), own_sem.at[2, g, 1])
 
+    holders = (me, partner)
+    ends = [(et0_ref.at[i], et_ref.at[i]) for i in range(2)]
+    end_final = (ef0_ref, ef_ref)
+
+    def cross_end(g, i):
+        first = (half * CELLS, far)[i]
+        src, dst = group(made, g, first, CELLS), group(ends[i], g, 0, CELLS)
+        return remote(src, dst, es_sem.at[i, g], er_sem.at[i, g], holders[i], other)
+
+    def relay_end(g, i, to):
+        src, dst = group(ends[i], g, to), group(end_final, g, holders[i])
+        return remote(src, dst, fs2_sem.at[i, g], fr2_sem.at[i, g], half * CELLS + to)
+
+    def all_end(i, g):
+        some = group(end_final, g, 0, CELLS - 1)
+        return remote(some, some, fs2_sem.at[i, g], fr2_sem.at[i, g], partner)
+
+    def keep_end(g, i):
+        return pltpu.make_async_copy(group(ends[i], g, cell), group(end_final, g, holders[i]), ek_sem.at[i, g])
+
+    def store_end(x):
+        return pltpu.make_async_copy(e_ref.at[x], n_hbm.at[1 - tm // 7, x], ek_sem.at[2, x])
+
     def send_back(g):
         cross_back(g).start()
         each_cell(lambda to: spread_back(g, to).start())
@@ -405,6 +445,9 @@
         cross(q, x).start()
         each_cell(lambda to: spread(q, x, to).start())
         keep(q, x).start()
+
+    for copy in loads[:2]:
+        copy.wait()
 
     @pl.loop(0, 3)
     def _(x):
@@ -416,7 +459,11 @@
         def _(c):
             rows_step(z_ref, fy, x, c, s_ref)
 
-        @pl.when(x == 0)
+        @pl.when((x == 0) & at_end)
+        def _():
+            pl.semaphore_wait(barrier, CELLS + 3)
+
+        @pl.when((x == 0) & jnp.logical_not(at_end))
         def _():
             pl.semaphore_wait(barrier, CELLS + 2)
 
@@ -428,6 +475,8 @@
 
     every = pl.ds(0, 24 * (CELLS - 1))
     weights_step(pairs_ref, signs_ref, w_ref)
+    for copy in loads[2:]:
+        copy.wait()
 
     @pl.loop(0, 3)
     def _(q):
@@ -471,9 +520,45 @@
         for pair in range(2):
             rows_back_step(cr0_ref, cr_ref, iy, x, pair, g_ref)
         depth_back_step(g_ref, iz, x, o_ref)
-        for k in range(2):
-            time_copy(k, x).start()
+
+        @pl.when(tm > 0)
+        def _():
+            time_copy(0, x).start()
+
+        @pl.when(tm < 7)
+        def _():
+            time_copy(1, x).start()
+
         store(x).start()
+
+    @pl.when(at_end)
+    def _():
+        for g in range(3):
+            for i in (1, 0):
+                cross_end(g, i).start()
+
+    @pl.when(at_end)
+    def _():
+        for g in range(3):
+            for i in (1, 0):
+                cross_end(g, i).wait_recv()
+                each_cell(lambda to: relay_end(g, i, to).start())
+                keep_end(g, i).start()
+        for g in range(3):
+            for i in range(2):
+                all_end(i, g).wait_recv()
+                keep_end(g, i).wait()
+        for x in range(3):
+            for pair in range(2):
+                rows_back_step(ef0_ref, ef_ref, iy, x, pair, g_ref)
+            depth_back_step(g_ref, iz, x, e_ref)
+            store_end(x).start()
+        for x in range(3):
+            store_end(x).wait()
+        for g in range(3):
+            for i in range(2):
+                all_end(i, g).wait_send()
+                cross_end(g, i).wait_send()
 
     for i in range(2):
         remote(s_ref.at[:, :, every], s_ref.at[:, :, every], fs_sem.at[i], fr_sem.at[i, 0], partner).wait_send()
@@ -486,10 +571,17 @@
     def _(q):
         for x in range(3):
             cross(q, x).wait_send()
-        for k in range(2):
-            time_copy(k, q).wait_send()
-            time_copy(k, q).wait_recv()
         store(q).wait()
+
+        @pl.when(tm > 0)
+        def _():
+            time_copy(0, q).wait_send()
+            time_copy(1, q).wait_recv()
+
+        @pl.when(tm < 7)
+        def _():
+            time_copy(1, q).wait_send()
+            time_copy(0, q).wait_recv()
 
 
 def per_device(field_a, field_b, pairs, signs):
@@ -500,7 +592,7 @@
     own, others = pl.pallas_call(
         whole_kernel,
         out_shape=[jax.ShapeDtypeStruct((3, 192, 384), F32), jax.ShapeDtypeStruct((2, 3, 192, 384), F32)],
-        in_specs=[ANY, ANY, SMEM, SMEM] + [VMEM] * 6,
+        in_specs=[ANY, ANY, SMEM, SMEM] + [ANY] * 6,
         out_specs=[ANY] * 2,
         scratch_shapes=[
             pltpu.VMEM((2, 3, 8, 18432), F32),
@@ -518,8 +610,20 @@
             pltpu.VMEM((2, CELLS * 24, 128), F32),
             pltpu.VMEM((PEERS * 8, 128), F32),
             pltpu.VMEM((2, PEERS * 24, 128), F32),
+            pltpu.VMEM((2, CELLS * 8, 128), F32),
+            pltpu.VMEM((2, 2, CELLS * 24, 128), F32),
+            pltpu.VMEM((PEERS * 8, 128), F32),
+            pltpu.VMEM((2, PEERS * 24, 128), F32),
             pltpu.VMEM((3, 4, 192, 128), F32),
             pltpu.VMEM((3, 192, 384), F32),
+            pltpu.VMEM((3, 192, 384), F32),
+            pltpu.VMEM(fz.shape, BF16),
+            pltpu.VMEM(fy.shape, BF16),
+            pltpu.VMEM(fx.shape, BF16),
+            pltpu.VMEM(ix.shape, BF16),
+            pltpu.VMEM(iy.shape, BF16),
+            pltpu.VMEM(iz.shape, BF16),
+            dma((6,)),
             dma((2, 3)),
             dma((3,)),
             dma((3, 3, 3)),
@@ -533,6 +637,11 @@
             dma((2, 3)),
             dma((2, 3)),
             dma((2, 3)),
+            dma((2, 3)),
+            dma((2, 3)),
+            dma((2, 3)),
+            dma((2, 3)),
+            dma((3, 3)),
         ],
         compiler_params=pltpu.CompilerParams(vmem_limit_bytes=60_000_000, collective_id=0, has_side_effects=True),
         name="whole",

time: 141 us -> 140 us (level); the launches traced: 141 us -> 138 us
  Pallas kernels: 141 us -> 137 us
    pallas_call x1, Pallas kernels: 138 us -> 134 us  [per_device(): pl.pallas_call(whole_kernel, out_shape=[jax.ShapeDtypeStruct((3, 192, 384...]
where the time goes in v5:
time: 140 us; the launch traced here: 138 us
  Pallas kernels  137 us (98%)
    pallas_call x1, Pallas kernels, per_device(): pl.pallas_call(whole_kernel, out_shape=[jax.ShapeDtypeStruct((3, 192, 384...  134 us
    pallas_call x1, Pallas kernels, per_device(): pl.pallas_call(differences_kernel, out_shape=[jax.ShapeDtypeStruct((3, 4,...  2.87 us

profile of v5, /device:TPU:1, one launch (start us, length us, event | category | flops | bytes accessed | tf_op | source)
XLA Modules:
  0.0 138.0 jit_solution(2492742862324393809)
XLA Ops:
  0.6 134.5 %whole.1 = (f32[3,192,384]{2,1,0:T(8,128)}, f32[2,3,192,384]{3,2,1,0:T(8,128)}) custom-call(f32[3,8,18432]{2,1,0:T(8,128)} %bitcast.16, f32[3,8,18432]{2,1,0:T(8,128)} %bitcast.17, s32[4,2,16]{2,1,0:T(2,128)} %bitcast.18, s32[4,16]{1,0:T(4,128)} %signs_ref.1, bf16[2,2,256,256]{3,2,1,0:T(8,128)(2,1)} %constant.12.clone.fz_hbm, ...), custom_call_target="tpu_custom_call" | custom-call | tf_op jit(solution)/shard_map/whole/pallas_call | solution.py:592
  135.1 2.9 %differences.1 = (f32[3,4,18432]{2,1,0:T(4,128)}, f32[3,4,18432]{2,1,0:T(4,128)}, f32[3,4,18432]{2,1,0:T(4,128)}) custom-call(f32[3,192,384]{2,1,0:T(8,128)} %get-tuple-element.8.o_hbm, f32[2,3,192,384]{3,2,1,0:T(8,128)} %get-tuple-element.9.n_hbm), custom_call_target="tpu_custom_call" | custom-call | tf_op jit(solution)/shard_map/differences/pallas_call | solution.py:649

commit v6 on v5

--- a/solution.py
+++ b/solution.py
@@ -506,6 +506,11 @@
             def _():
                 send_back(g)
 
+    @pl.when(at_end)
+    def _():
+        for g, i in ((0, 1), (1, 1), (2, 1)):
+            cross_end(g, i).start()
+
     for g in range(3):
         cross_back(g).wait_recv()
         each_cell(lambda to: relay_back(g, to).start())
@@ -533,17 +538,15 @@
 
     @pl.when(at_end)
     def _():
-        for g in range(3):
-            for i in (1, 0):
-                cross_end(g, i).start()
+        for g, i in ((0, 0), (1, 0), (2, 0)):
+            cross_end(g, i).start()
 
     @pl.when(at_end)
     def _():
-        for g in range(3):
-            for i in (1, 0):
-                cross_end(g, i).wait_recv()
-                each_cell(lambda to: relay_end(g, i, to).start())
-                keep_end(g, i).start()
+        for i, g in [(i, g) for i in (1, 0) for g in range(3)]:
+            cross_end(g, i).wait_recv()
+            each_cell(lambda to: relay_end(g, i, to).start())
+            keep_end(g, i).start()
         for g in range(3):
             for i in range(2):
                 all_end(i, g).wait_recv()

time: 140 us -> 138 us (0.986); the launches traced: 138 us -> 138 us
  no operation moved by 1% of the time
where the time goes in v6:
time: 138 us
  Pallas kernels  137 us (99%)
    pallas_call x1, Pallas kernels, per_device(): pl.pallas_call(whole_kernel, out_shape=[jax.ShapeDtypeStruct((3, 192, 384...  134 us
    pallas_call x1, Pallas kernels, per_device(): pl.pallas_call(differences_kernel, out_shape=[jax.ShapeDtypeStruct((3, 4,...  2.87 us

profile of v6, /device:TPU:1, one launch (start us, length us, event | category | flops | bytes accessed | tf_op | source)
XLA Modules:
  0.0 138.0 jit_solution(18006688740309992837)
XLA Ops:
  0.6 134.5 %whole.1 = (f32[3,192,384]{2,1,0:T(8,128)}, f32[2,3,192,384]{3,2,1,0:T(8,128)}) custom-call(f32[3,8,18432]{2,1,0:T(8,128)} %bitcast.16, f32[3,8,18432]{2,1,0:T(8,128)} %bitcast.17, s32[4,2,16]{2,1,0:T(2,128)} %bitcast.18, s32[4,16]{1,0:T(4,128)} %signs_ref.1, bf16[2,2,256,256]{3,2,1,0:T(8,128)(2,1)} %constant.12.clone.fz_hbm, ...), custom_call_target="tpu_custom_call" | custom-call | tf_op jit(solution)/shard_map/whole/pallas_call | solution.py:595
  135.1 2.9 %differences.1 = (f32[3,4,18432]{2,1,0:T(4,128)}, f32[3,4,18432]{2,1,0:T(4,128)}, f32[3,4,18432]{2,1,0:T(4,128)}) custom-call(f32[3,192,384]{2,1,0:T(8,128)} %get-tuple-element.8.o_hbm, f32[2,3,192,384]{3,2,1,0:T(8,128)} %get-tuple-element.9.n_hbm), custom_call_target="tpu_custom_call" | custom-call | tf_op jit(solution)/shard_map/differences/pallas_call | solution.py:652

commit v7 on v6

--- a/solution.py
+++ b/solution.py
@@ -158,7 +158,7 @@
         b_re = [h_ref[j, re, 128:] for j in range(8)]
         b_im = [h_ref[j, im, 128:] for j in range(8)]
 
-        @pl.loop(0, 4)
+        @pl.loop(0, 4, unroll=4)
         def _(ch):
             sum_re, sum_im = jnp.zeros((8, 128), F32), jnp.zeros((8, 128), F32)
             for i in range(8):
@@ -253,45 +253,50 @@
 ANY = pl.BlockSpec(memory_space=pl.ANY)
 
 
-def difference_step(o_ref, n_ref, out_ref, x):
-    for pair in range(24):
-        rows = pl.ds(pair * 8, 8)
+def difference_step(o_ref, n_ref, out_ref, x, third):
+    for pair in range(8):
+        rows = pl.ds(pl.multiple_of(third * 64 + pair * 8, 8), 8)
         now, later, earlier = o_ref[x, rows, :], n_ref[0, x, rows, :], n_ref[1, x, rows, :]
         first = later - now
         second = later - 2.0 * now + earlier
         for half in range(2):
-            at = pl.ds(pair * 768 + half * 384, 384)
+            at = pl.ds(pl.multiple_of(third * 6144 + pair * 768 + half * 384, 128), 384)
             out_ref[0, x, :, at] = now[4 * half : 4 * half + 4]
             out_ref[1, x, :, at] = first[4 * half : 4 * half + 4]
             out_ref[2, x, :, at] = second[4 * half : 4 * half + 4]
 
 
 def differences_kernel(o_hbm, n_hbm, c_hbm, f_hbm, d_hbm, o_ref, n_ref, out_ref, in_sem, out_sem):
-    def loads(x):
+    def loads(i):
+        x, rows = i // 3, pl.ds(pl.multiple_of(lax.rem(i, 3) * 64, 8), 64)
         return (
-            pltpu.make_async_copy(o_hbm.at[x], o_ref.at[x], in_sem.at[0, x]),
-            pltpu.make_async_copy(n_hbm.at[0, x], n_ref.at[0, x], in_sem.at[1, x]),
-            pltpu.make_async_copy(n_hbm.at[1, x], n_ref.at[1, x], in_sem.at[2, x]),
+            pltpu.make_async_copy(o_hbm.at[x, rows], o_ref.at[x, rows], in_sem.at[0, i]),
+            pltpu.make_async_copy(n_hbm.at[0, x, rows], n_ref.at[0, x, rows], in_sem.at[1, i]),
+            pltpu.make_async_copy(n_hbm.at[1, x, rows], n_ref.at[1, x, rows], in_sem.at[2, i]),
         )
 
-    def store(i, x):
-        return pltpu.make_async_copy(out_ref.at[i, x], (c_hbm, f_hbm, d_hbm)[i].at[x], out_sem.at[i, x])
-
-    for x in range(3):
-        for copy in loads(x):
+    def store(k, i):
+        x, at = i // 3, pl.ds(pl.multiple_of(lax.rem(i, 3) * 6144, 128), 6144)
+        out = (c_hbm, f_hbm, d_hbm)[k].at[x, :, at]
+        return pltpu.make_async_copy(out_ref.at[k, x, :, at], out, out_sem.at[k, i])
+
+    @pl.loop(0, 9)
+    def _(i):
+        for copy in loads(i):
             copy.start()
 
-    @pl.loop(0, 3)
-    def _(x):
-        for copy in loads(x):
+    @pl.loop(0, 9)
+    def _(i):
+        for copy in loads(i):
             copy.wait()
-        difference_step(o_ref, n_ref, out_ref, x)
-        for i in range(3):
-            store(i, x).start()
-
-    for x in range(3):
-        for i in range(3):
-            store(i, x).wait()
+        difference_step(o_ref, n_ref, out_ref, i // 3, lax.rem(i, 3))
+        for k in range(3):
+            store(k, i).start()
+
+    @pl.loop(0, 9)
+    def _(i):
+        for k in range(3):
+            store(k, i).wait()
 
 
 def whole_kernel(
@@ -658,8 +663,8 @@
             pltpu.VMEM((3, 192, 384), F32),
             pltpu.VMEM((2, 3, 192, 384), F32),
             pltpu.VMEM((3, 3, 4, 18432), F32),
-            dma((3, 3)),
-            dma((3, 3)),
+            dma((3, 9)),
+            dma((3, 9)),
         ],
         compiler_params=pltpu.CompilerParams(vmem_limit_bytes=62_000_000),
         name="differences",

time: 138 us -> 138 us (level)
  no operation moved by 1% of the time
where the time goes in v7:
time: 138 us
  Pallas kernels  138 us (100%)
    pallas_call x1, Pallas kernels, per_device(): pl.pallas_call(whole_kernel, out_shape=[jax.ShapeDtypeStruct((3, 192, 384...  134 us
    pallas_call x1, Pallas kernels, per_device(): pl.pallas_call(differences_kernel, out_shape=[jax.ShapeDtypeStruct((3, 4,...  3.07 us

profile of v7, /device:TPU:1, one launch (start us, length us, event | category | flops | bytes accessed | tf_op | source)
XLA Modules:
  0.0 138.2 jit_solution(7167361825670892302)
XLA Ops:
  0.6 134.5 %whole.1 = (f32[3,192,384]{2,1,0:T(8,128)}, f32[2,3,192,384]{3,2,1,0:T(8,128)}) custom-call(f32[3,8,18432]{2,1,0:T(8,128)} %bitcast.16, f32[3,8,18432]{2,1,0:T(8,128)} %bitcast.17, s32[4,2,16]{2,1,0:T(2,128)} %bitcast.18, s32[4,16]{1,0:T(4,128)} %signs_ref.1, bf16[2,2,256,256]{3,2,1,0:T(8,128)(2,1)} %constant.12.clone.fz_hbm, ...), custom_call_target="tpu_custom_call" | custom-call | tf_op jit(solution)/shard_map/whole/pallas_call | solution.py:600
  135.1 3.1 %differences.1 = (f32[3,4,18432]{2,1,0:T(4,128)}, f32[3,4,18432]{2,1,0:T(4,128)}, f32[3,4,18432]{2,1,0:T(4,128)}) custom-call(f32[3,192,384]{2,1,0:T(8,128)} %get-tuple-element.8.o_hbm, f32[2,3,192,384]{3,2,1,0:T(8,128)} %get-tuple-element.9.n_hbm), custom_call_target="tpu_custom_call" | custom-call | tf_op jit(solution)/shard_map/differences/pallas_call | solution.py:657
